TPU v7x, 512 devices: a whole 4x8x8 slice. The times are simulated.
512 devices in a mesh: ctx: 32 (over z, x), ch: 16 (over y, core).
Axes of the slice: x: 4, y: 8, z: 8, core: 2. Of those that a mesh axis runs over, the one named last changes fastest.
Arguments:
- query_seq: bfloat16 [4096, 4096], P('ctx', 'ch'), may hold values from -6 to 6
- key_seq: bfloat16 [4096, 4096], P('ctx', 'ch'), may hold values from -6 to 6
- value_seq: bfloat16 [4096, 4096], P('ctx', 'ch'), may hold values from -6 to 6
- out_grad: bfloat16 [4096, 4096], P('ctx', 'ch'), may hold values from -6 to 6
- filters: bfloat16 [4096, 256], P('ctx', 'ch'), may hold values from -6 to 6
- skip_gain: float32 [4096], P('ch'), may hold values from -1 to 1
- reaches: int32 [256], P('ch'), may hold values from 1 to 32, as said below
Outputs:
- mixed: bfloat16 [4096, 4096], P('ctx', 'ch')
- query_grad: bfloat16 [4096, 4096], P('ctx', 'ch')
- key_grad: bfloat16 [4096, 4096], P('ctx', 'ch')
- value_grad: bfloat16 [4096, 4096], P('ctx', 'ch')
- filter_grad: float32 [4096, 256], P('ctx', 'ch')
- skip_grad: float32 [4096], P('ch')
Inputs may be any that keep to these rules, and one draw needn't show every extreme that they name: Each group's reach counts its own span; some group reaches the whole context and some group only its own span.
All inputs are finite; a program needn't handle non-finite values.
Results may differ from a plain program's by a relative error of at most 0.01.
Values may be sent and summed in bfloat16 or wider, within the bound.
No kernel may reach another device: no remote copies, remote signals or barrier semaphores. Data moves between devices by JAX's collectives and lax.ppermute only.
A program may use at most 64 MiB of HBM per device.

v0:
```python
import math

import jax
import jax.numpy as jnp
from jax import lax
from jax.sharding import PartitionSpec as P

GROUP = 16


def toeplitz(window):
    size_two, groups = window.shape
    block_len = size_two // 2
    flipped = window[::-1].T
    tiled = jnp.tile(flipped, (1, block_len))
    shaped = tiled[:, : block_len * (2 * block_len - 1)].reshape(
        groups, block_len, 2 * block_len - 1
    )
    return shaped[:, :, block_len - 1 :]


def diag_sum(prods):
    groups, block_len, _ = prods.shape
    padded = jnp.pad(prods, ((0, 0), (0, 0), (block_len - 1, 0)))
    flat = padded.reshape(groups, block_len * (2 * block_len - 1))
    flat = jnp.pad(flat, ((0, 0), (0, block_len)))
    sums = flat.reshape(groups, block_len, 2 * block_len).sum(axis=1)
    return sums[:, ::-1].T


def add_window(tap_sums, window_grad, offset, block_len):
    current = lax.dynamic_slice_in_dim(tap_sums, offset * block_len, 2 * block_len, 0)
    return lax.dynamic_update_slice_in_dim(tap_sums, current + window_grad, offset * block_len, 0)


def kernel_block(taps, limits, offset, block_len):
    window = lax.dynamic_slice_in_dim(taps, offset * block_len, 2 * block_len, 0)
    weights = offset < limits
    tmat = toeplitz(window) * weights.astype(jnp.bfloat16)[:, None, None]
    return (tmat, weights.astype(jnp.float32))


def body(query_seq, key_seq, value_seq, out_grad, filters, skip_gain, reaches):
    f32 = jnp.float32
    block_len = query_seq.shape[0]
    local_width = query_seq.shape[1]
    local_groups = local_width // GROUP
    num_spans = lax.axis_size("ctx")
    seq_len = block_len * num_spans
    scale = 1.0 / math.sqrt(seq_len)
    myself = lax.axis_index("ctx")
    z_vals = (key_seq.astype(f32) * value_seq.astype(f32)).astype(jnp.bfloat16)
    grads = (out_grad.astype(f32) * query_seq.astype(f32)).astype(jnp.bfloat16)
    all_taps = lax.all_gather(filters, "ctx", axis=0, tiled=True)
    taps = jnp.concatenate([jnp.zeros((block_len, local_groups), jnp.bfloat16), all_taps], axis=0)
    longest = jnp.max(reaches)
    own_grads = grads.reshape(block_len, local_groups, GROUP)
    start = (
        jnp.zeros((block_len, local_groups, GROUP), f32),
        jnp.zeros((block_len, local_groups, GROUP), f32),
        jnp.zeros((seq_len + block_len, local_groups), f32),
    )
    z_piece = lax.all_gather(z_vals, "ctx", axis=0, tiled=True)
    g_piece = lax.all_gather(grads, "ctx", axis=0, tiled=True)
    count = z_piece.shape[0] // block_len

    def span_step(position, state):
        filtered, back_sum, tap_sums = state
        remote_z = lax.dynamic_slice_in_dim(z_piece, position * block_len, block_len, 0)
        remote_z = remote_z.reshape(block_len, local_groups, GROUP)
        remote_g = lax.dynamic_slice_in_dim(g_piece, position * block_len, block_len, 0)
        remote_g = remote_g.reshape(block_len, local_groups, GROUP)
        ahead = myself - position
        behind = position - myself

        def forward(inner):
            acc, sums = inner
            tmat, weights = kernel_block(taps, reaches, ahead, block_len)
            acc = acc + jnp.einsum("gab,bgc->agc", tmat, remote_z, preferred_element_type=f32)
            prods = jnp.einsum("agc,bgc->gab", own_grads, remote_z, preferred_element_type=f32)
            prods = prods * weights[:, None, None]
            return (acc, add_window(sums, diag_sum(prods), ahead, block_len))

        filtered, tap_sums = lax.cond(
            (ahead >= 0) & (ahead < longest), forward, lambda inner: inner, (filtered, tap_sums)
        )

        def backward(acc):
            tmat, weights = kernel_block(taps, reaches, behind, block_len)
            return acc + jnp.einsum("gab,agc->bgc", tmat, remote_g, preferred_element_type=f32)

        back_sum = lax.cond((behind >= 0) & (behind < longest), backward, lambda acc: acc, back_sum)
        return (filtered, back_sum, tap_sums)

    filtered, back_sum, tap_sums = lax.fori_loop(0, count, span_step, start)
    filtered = filtered.reshape(block_len, local_width)
    back_sum = back_sum.reshape(block_len, local_width)
    filter_grad = (
        lax.psum_scatter(tap_sums[block_len:], "ctx", scatter_dimension=0, tiled=True) * scale
    )
    skip_grad = lax.psum(jnp.sum(grads.astype(f32) * z_vals.astype(f32), axis=0), "ctx")
    filtered = filtered * scale
    back_sum = back_sum * scale
    total = filtered + skip_gain[None, :] * z_vals.astype(f32)
    mixed = (query_seq.astype(f32) * total).astype(jnp.bfloat16)
    query_grad = (out_grad.astype(f32) * total).astype(jnp.bfloat16)
    back_total = back_sum + skip_gain[None, :] * grads.astype(f32)
    key_grad = (back_total * value_seq.astype(f32)).astype(jnp.bfloat16)
    value_grad = (back_total * key_seq.astype(f32)).astype(jnp.bfloat16)
    return (mixed, query_grad, key_grad, value_grad, filter_grad, skip_grad)


def solution(mesh):
    in_specs = (
        P("ctx", "ch"),
        P("ctx", "ch"),
        P("ctx", "ch"),
        P("ctx", "ch"),
        P("ctx", "ch"),
        P("ch"),
        P("ch"),
    )
    out_specs = (
        P("ctx", "ch"),
        P("ctx", "ch"),
        P("ctx", "ch"),
        P("ctx", "ch"),
        P("ctx", "ch"),
        P("ch"),
    )
    return jax.shard_map(body, mesh=mesh, in_specs=in_specs, out_specs=out_specs, check_vma=False)
```

profile of v0, /device:TPU:56, one launch (start us, length us, event | category | flops | bytes accessed | tf_op | source)
XLA Modules:
  0.0 959.2 jit_solution(9368183063505255978)
XLA Ops:
  14.0 55.2 %all_gather.9 = bf16[4096,16]{0,1:T(8,128)(2,1)S(1)} all-gather(bf16[128,16]{0,1:T(8,128)(2,1)} %param.17), channel_id=1, replica_groups=mesh['ctx'=32,'ch'=16] {'ctx'}, dimensions={0}, use_global_device_ids=true | all-gather | bytes 135168 | tf_op jit(solution)/shard_map/all_gather | solution.py:54
  69.9 27.5 %all-gather.3.cloned.1.call-done = bf16[4096,256]{0,1:T(8,128)(2,1)} async-done(((bf16[128,256]{0,1:T(8,128)(2,1)}), bf16[4096,256]{0,1:T(8,128)(2,1)}) %all-gather.3.cloned.1.call-update) | async-done | bytes 2097168 | tf_op jit(solution)/shard_map/all_gather | solution.py:63
  97.4 83.6 %all-gather.5.cloned.1.call-done = bf16[4096,256]{0,1:T(8,128)(2,1)} async-done(((bf16[128,256]{0,1:T(8,128)(2,1)}), bf16[4096,256]{0,1:T(8,128)(2,1)}) %all-gather.5.cloned.1.call-update) | async-done | bytes 2097168 | tf_op jit(solution)/shard_map/all_gather | solution.py:64
  181.7 326.7 %while.20 = (s32[]{:T(128)}, f32[128,16,16]{0,2,1:T(8,128)S(1)}, f32[128,16,16]{0,2,1:T(8,128)}, f32[4224,16]{0,1:T(8,128)S(1)}, s32[]{:T(128)}, /*index=5*/s32[...) while((s32[]{:T(128)}, f32[128,16,16]{0,2,1:T(8,128)S(1)}, ...), condition=%wide.region_7.8_spmd, body=%wide.region_1.7_spmd.sunk | while | flops 27328612 | bytes 39176128 | solution.py:95
  183.0 8.4 conditional.5
  191.4 15.6 %conditional.4 = ((f32[128,16,16]{0,2,1:T(8,128)S(1)}, f32[4224,16]{0,1:T(8,128)S(1)})) conditional(s32[]{:T(128)} %convert_element_type.145, (f32[128,16,16]{0,2,1:T(8,128)S(1)}, f32[4224,16]{0,1:T(8,128)S(1)}) %tuple.66, (s32[]{:T(128)}, bf16[4224,16]{0,1:T(8,128)(2,1)}, s32[16]{0:T(128)}, bf16[4096,256]{0,1:T(8,128)(2,1)}, s32[]{:T(128)}, ...), branch_computations={%region_2.0_spmd, %region_3.4_spmd} | conditional | flops 17858612 | bytes 30565238 | solution.py:84
  208.3 8.4 conditional.5
  218.0 8.4 conditional.5
  227.7 8.4 conditional.5
  237.5 8.4 conditional.5
  247.2 8.4 conditional.5
  256.9 8.4 conditional.5
  266.6 8.4 conditional.5
  276.4 8.4 conditional.5
  286.1 8.4 conditional.5
  295.8 8.4 conditional.5
  305.5 8.4 conditional.5
  315.2 8.4 conditional.5
  325.0 8.4 conditional.5
  334.7 8.4 conditional.5
  422.2 8.4 conditional.5
  461.1 8.4 conditional.5
  509.2 321.6 %psum.7 = f32[256]{0:T(256)} all-reduce(f32[256]{0:T(256)S(1)} %get-tuple-element.328), channel_id=1, replica_groups=mesh['ctx'=32,'ch'=16] {'ctx'}, use_global_device_ids=true, to_apply=%region_10.11 | all-reduce | flops 256 | bytes 2048 | tf_op jit(solution)/shard_map/psum | solution.py:101
  835.8 115.6 %reduce-scatter.2.cloned.1.call-done = f32[128,16]{0,1:T(8,128)} async-done(((f32[4096,16]{0,1:T(8,128)}), f32[128,16]{0,1:T(8,128)}) %reduce-scatter.2.cloned.1.call-update) | async-done | bytes 8208 | tf_op jit(solution)/shard_map/reduce_scatter | solution.py:99
  (454 shorter events, 426.7 us)
Async XLA Ops:
  7.2 90.2 %all-gather.3.cloned.1.call-start = ((), (), s32[]{:S(2)}) async-start(), calls=%async_computation.1 | async-start | bytes 2162688 | tf_op jit(solution)/shard_map/all_gather | solution.py:63
  8.2 173.5 %copy-start.1 = (bf16[128,256]{0,1:T(8,128)(2,1)}, bf16[128,256]{0,1:T(8,128)(2,1)S(1)}, u32[]{:S(2)}) copy-start(bf16[128,256]{0,1:T(8,128)(2,1)S(1)} %copy.19) | copy-start | bytes 196612
  9.2 172.5 %copy-start.2 = (bf16[128,256]{0,1:T(8,128)(2,1)}, bf16[128,256]{0,1:T(8,128)(2,1)S(1)}, u32[]{:S(2)}) copy-start(bf16[128,256]{0,1:T(8,128)(2,1)S(1)} %copy.20) | copy-start | bytes 196612
  10.2 171.5 %copy-start.3 = (bf16[128,256]{0,1:T(8,128)(2,1)}, bf16[128,256]{0,1:T(8,128)(2,1)S(1)}, u32[]{:S(2)}) copy-start(bf16[128,256]{0,1:T(8,128)(2,1)S(1)} %copy.21) | copy-start | bytes 196612
  11.1 170.5 %copy-start.4 = (bf16[128,256]{0,1:T(8,128)(2,1)}, bf16[128,256]{0,1:T(8,128)(2,1)S(1)}, u32[]{:S(2)}) copy-start(bf16[128,256]{0,1:T(8,128)(2,1)S(1)} %copy.22) | copy-start | bytes 196612
  11.9 169.1 %all-gather.5.cloned.1.call-start = ((), (), s32[]{:S(2)}) async-start(), calls=%async_computation.2 | async-start | bytes 2162688 | tf_op jit(solution)/shard_map/all_gather | solution.py:64
  12.6 938.8 %reduce-scatter.2.cloned.1.call-start = ((), (), s32[]{:S(2)}) async-start(), calls=%async_computation.3 | async-start | bytes 270336 | tf_op jit(solution)/shard_map/reduce_scatter | solution.py:99
  181.7 650.0 %copy-start.7 = (f32[256]{0:T(256)S(1)}, f32[256]{0:T(256)}, u32[]{:S(2)}) copy-start(f32[256]{0:T(256)} %param.18) | copy-start | bytes 3076
  208.3 8.5 copy-start
  218.0 8.5 copy-start
  227.7 8.5 copy-start
  237.4 8.5 copy-start
  247.2 8.5 copy-start
  256.9 8.5 copy-start
  266.6 8.5 copy-start
  286.1 8.5 copy-start
  295.8 8.5 copy-start
  305.5 8.5 copy-start
  315.2 8.5 copy-start
  325.0 8.5 copy-start
  334.7 8.5 copy-start
  354.1 8.5 copy-start
  363.8 8.5 copy-start
  461.1 8.5 copy-start
  (18 other events, 138.7 us)
Sparse Core Ops, SparseCore 0:
  12.0 85.3 all-gather.2
  101.0 79.9 all-gather.4
  509.3 442.0 reduce-scatter.1
where the time goes:
time: 968 us; the launch traced here: 959 us
  blocking collectives  377 us (39%)
  waiting for transfers between devices  227 us (23%)
  local copies, waits for them, and re-layouts  208 us (21%)
  matrix products  63.8 us (7%)
  loops' own time  42 us (4%)
  other arithmetic  27.4 us (3%)
  between operations  13.9 us (1%)
    psum x1, blocking collectives, body(): lax.psum(jnp.sum(grads.astype(f32) * z_vals.astype(f32), axis=0), 'ctx')  322 us
    reduce_scatter x1, waiting for transfers between devices, body(): lax.psum_scatter(tap_sums[block_len:], 'ctx', scatter_dimension=0, tiled=...  116 us
    reshape x33, local copies, waits for them, and re-layouts, toeplitz(): tiled[:, :block_len * (2 * block_len - 1)]  112 us
    all_gather x1, waiting for transfers between devices, body(): g_piece = lax.all_gather(grads, 'ctx', axis=0, tiled=True)  83.6 us
    dot_general x32, matrix products, backward(): jnp.einsum('gab,agc->bgc', tmat, remote_g, preferred_element_type=f32)  61.4 us
    all_gather x1, blocking collectives, body(): all_taps = lax.all_gather(filters, 'ctx', axis=0, tiled=True)  55.2 us
    another operation x1, loops' own time, body(): filtered, back_sum, tap_sums = lax.fori_loop(0, count, span_step, start)  40.6 us
    all_gather x1, waiting for transfers between devices, body(): z_piece = lax.all_gather(z_vals, 'ctx', axis=0, tiled=True)  27.5 us
  transfers between devices with their start and end apart: 3, of which 3 were waited for; matrix products, arithmetic and copies ran while one was open for 1% of the time, Pallas kernels for 0%

commit v1 on v0

v1 whole, which is shorter than its diff:
```python
import math

import jax
import jax.numpy as jnp
from jax import lax
from jax.experimental import pallas as pl
from jax.experimental.pallas import tpu as pltpu
from jax.sharding import PartitionSpec as P

GROUP = 16
ROWS = 24
F32 = jnp.float32
BF16 = jnp.bfloat16


def eye(size, flip):
    row = lax.broadcasted_iota(jnp.int32, (size, size), 0)
    col = lax.broadcasted_iota(jnp.int32, (size, size), 1)
    hit = (row + col == size - 1) if flip else (row == col)
    return jnp.where(hit, 1.0, 0.0).astype(BF16)


def matmul(lhs, rhs):
    return jnp.dot(lhs, rhs, preferred_element_type=F32)


def matmul_nt(lhs, rhs):
    return lax.dot_general(lhs, rhs, (((1,), (1,)), ((), ())), preferred_element_type=F32)


def product(first, second):
    return (first.astype(F32) * second.astype(F32)).astype(BF16)


def pack_body(query, key, value, cotangent, taps, packed):
    spans = packed.shape[0]
    block_len = query.shape[0]
    z_rows = product(key[...], value[...]).astype(F32).T
    g_rows = product(cotangent[...], query[...]).astype(F32).T
    tap_rows = taps[...].astype(F32)
    for dest in range(spans):
        group = dest * 8 // GROUP
        tail = jnp.broadcast_to(tap_rows[group : group + 1], (8, block_len))
        tile = jnp.concatenate(
            [z_rows[dest * 8 : dest * 8 + 8], g_rows[dest * 8 : dest * 8 + 8], tail], axis=0
        )
        packed[dest] = tile.astype(BF16)


def conv_body(reaches, packed, out, toep, shifted):
    spans, _, block_len = packed.shape
    wide = 2 * block_len
    half = spans // 2
    reach = reaches[lax.axis_index("ctx") * 8 // GROUP]
    row = lax.broadcasted_iota(jnp.int32, (block_len, block_len), 0)
    col = lax.broadcasted_iota(jnp.int32, (block_len, block_len), 1)
    upper = col >= row
    flip = eye(block_len, True)

    tiles = [packed[span].astype(F32) for span in range(spans)]
    z_list = [tile[0:8] for tile in tiles]
    g_list = [tile[8:16] for tile in tiles]
    weights = [(offset < reach).astype(F32) for offset in range(spans)]

    toep[:, 0:block_len] = jnp.zeros((block_len, block_len), BF16)
    before = jnp.zeros((block_len, block_len), F32)
    for offset in range(spans):
        window = jnp.broadcast_to(tiles[offset][16:17], (block_len, block_len))
        turned = pltpu.roll(window, 0, 1, stride=1, stride_axis=0)
        block = jnp.where(upper, turned, before) * weights[offset]
        toep[:, (offset + 1) * block_len : (offset + 2) * block_len] = block.astype(BF16)
        before = turned

    g_all = jnp.concatenate(g_list, axis=0).astype(BF16)
    g_flip = matmul(g_all, flip)

    parts = []
    for pair in range(half):
        first = 2 * pair
        parts.append(jnp.concatenate([z_list[first], z_list[first + 1]], axis=1))
        low, high = (spans - 1 - first) * 8, (spans - 2 - first) * 8
        parts.append(jnp.concatenate([g_flip[low : low + 8], g_flip[high : high + 8]], axis=1))
    data = jnp.concatenate(parts, axis=0).astype(BF16)
    acc = None
    for offset in range(half):
        base = 2 * offset * block_len
        block = jnp.concatenate(
            [toep[:, base + block_len : base + block_len + wide], toep[:, base : base + wide]], axis=0
        )
        term = matmul(data[: (half - offset) * 16], block)
        if acc is None:
            acc = term
        else:
            acc = jnp.concatenate([acc[: offset * 16], acc[offset * 16 :] + term], axis=0)

    z_flip = matmul(jnp.concatenate(z_list, axis=0).astype(BF16), flip)
    z_down = jnp.concatenate([jnp.zeros((8, block_len), F32), z_flip[:-8]], axis=0)
    shifted[0 : spans * 8] = jnp.zeros((spans * 8, wide), BF16)
    shifted[spans * 8 : spans * 16] = jnp.concatenate([z_flip, z_down], axis=1).astype(BF16)
    g_turn = jnp.concatenate(g_list, axis=0).T.astype(BF16)
    turned = []
    for pair in range(half):
        start = spans * 8 - 16 * pair
        prods = matmul(g_turn, shifted[start : start + spans * 8])
        for side in range(2):
            own = prods[:, side * block_len : (side + 1) * block_len] * weights[2 * pair + side]
            turned.append(pltpu.roll(own, 1, 1, stride=1, stride_axis=0))
    turned.append(jnp.zeros((block_len, block_len), F32))

    skip = jnp.zeros((8, block_len), F32)
    for span in range(spans):
        skip = skip + z_list[span] * g_list[span]
    skip = jnp.sum(skip, axis=1, keepdims=True)
    lane = lax.broadcasted_iota(jnp.int32, (8, block_len), 1)
    sub = lax.broadcasted_iota(jnp.int32, (8, block_len), 0)
    skip_row = jnp.sum(jnp.where(lane % 8 == sub, skip, 0.0), axis=0, keepdims=True)
    skip_high = skip_row.astype(BF16).astype(F32)
    skip_low = skip_row - skip_high

    for span in range(spans):
        pair, side = span // 2, span % 2
        forth = acc[pair * 16 : pair * 16 + 8, side * block_len : (side + 1) * block_len]
        mirror = spans - 1 - span
        pair, side = mirror // 2, mirror % 2
        back = acc[pair * 16 + 8 : pair * 16 + 16, side * block_len : (side + 1) * block_len]
        sums = jnp.sum(jnp.where(col <= row, turned[span], turned[span + 1]), axis=0, keepdims=True)
        high = sums.astype(BF16).astype(F32)
        low = sums - high
        tail = jnp.where(
            sub == 0, high, jnp.where(sub == 1, low, jnp.where(sub == 2, skip_high, skip_low))
        )
        out[span] = jnp.concatenate([forth, back, tail], axis=0).astype(BF16)


def gate_body(scale, query, key, value, cotangent, gain, packed, mixed, query_grad, key_grad, value_grad, tap_grad, skip_grad):
    spans, _, block_len = packed.shape
    tiles = [packed[span].astype(F32) for span in range(spans)]
    forth = jnp.concatenate([tile[0:8] for tile in tiles], axis=0).astype(BF16)
    back = jnp.concatenate([tile[8:16] for tile in tiles], axis=0).astype(BF16)
    flip = eye(block_len, True)
    filtered = matmul_nt(eye(block_len, False), forth) * scale
    back_sum = matmul_nt(flip, back) * scale
    q_val, k_val = query[...].astype(F32), key[...].astype(F32)
    v_val, o_val = value[...].astype(F32), cotangent[...].astype(F32)
    z_val = (k_val * v_val).astype(BF16).astype(F32)
    g_val = (o_val * q_val).astype(BF16).astype(F32)
    total = filtered + gain[...] * z_val
    mixed[...] = (q_val * total).astype(BF16)
    query_grad[...] = (o_val * total).astype(BF16)
    back_total = back_sum + gain[...] * g_val
    key_grad[...] = (back_total * v_val).astype(BF16)
    value_grad[...] = (back_total * k_val).astype(BF16)

    per_group = GROUP // 8
    for group in range(spans // per_group):
        rows = tiles[group * per_group][16:24]
        both = [rows[0:1], rows[1:2]]
        for member in range(1, per_group):
            rows = tiles[group * per_group + member][16:24]
            both = [both[0] + rows[0:1], both[1] + rows[1:2]]
        tap_grad[group : group + 1] = (both[0] + both[1]) * scale

    lane = lax.broadcasted_iota(jnp.int32, (1, block_len), 1)
    for part in range(skip_grad.shape[1] // block_len):
        line = jnp.zeros((1, block_len), F32)
        for place in range(block_len // 8):
            rows = tiles[part * (block_len // 8) + place][16:24]
            line = jnp.where(lane // 8 == place, rows[2:3] + rows[3:4], line)
        skip_grad[:, part * block_len : (part + 1) * block_len] = line


def whole(space=pltpu.VMEM):
    return pl.BlockSpec(memory_space=space)


def body(query_seq, key_seq, value_seq, out_grad, filters, skip_gain, reaches):
    block_len, local_width = query_seq.shape
    spans = lax.axis_size("ctx")
    local_groups = local_width // GROUP
    scale = 1.0 / math.sqrt(block_len * spans)
    packed_shape = jax.ShapeDtypeStruct((spans, ROWS, block_len), BF16)
    params = pltpu.CompilerParams(vmem_limit_bytes=48 * 1024 * 1024)

    packed = pl.pallas_call(
        pack_body,
        out_shape=packed_shape,
        in_specs=[whole()] * 5,
        out_specs=whole(),
        compiler_params=params,
        name="pack",
    )(query_seq, key_seq, value_seq, out_grad, filters.T)
    packed = lax.all_to_all(packed, "ctx", 0, 0, tiled=True)
    packed = pl.pallas_call(
        conv_body,
        out_shape=packed_shape,
        in_specs=[whole(space=pltpu.SMEM), whole()],
        out_specs=whole(),
        scratch_shapes=[
            pltpu.VMEM((block_len, (spans + 1) * block_len), BF16),
            pltpu.VMEM((spans * 16, 2 * block_len), BF16),
        ],
        compiler_params=params,
        name="conv",
    )(reaches, packed)
    packed = lax.all_to_all(packed, "ctx", 0, 0, tiled=True)
    act = jax.ShapeDtypeStruct((block_len, local_width), BF16)
    mixed, query_grad, key_grad, value_grad, tap_grad, skip_grad = pl.pallas_call(
        lambda *refs: gate_body(scale, *refs),
        out_shape=(
            act,
            act,
            act,
            act,
            jax.ShapeDtypeStruct((local_groups, block_len), F32),
            jax.ShapeDtypeStruct((1, local_width), F32),
        ),
        in_specs=[whole()] * 6,
        out_specs=[whole()] * 6,
        compiler_params=params,
        name="gate",
    )(query_seq, key_seq, value_seq, out_grad, skip_gain[None, :], packed)
    return (mixed, query_grad, key_grad, value_grad, tap_grad.T, skip_grad[0])


def solution(mesh):
    spec = P("ctx", "ch")
    return jax.shard_map(
        body,
        mesh=mesh,
        in_specs=(spec, spec, spec, spec, spec, P("ch"), P("ch")),
        out_specs=(spec, spec, spec, spec, spec, P("ch")),
        check_vma=False,
    )
```

time: 968 us -> 48.3 us (0.05)
  blocking collectives: 377 us -> 39.6 us
  waiting for transfers between devices: 227 us -> 0 us
  local copies, waits for them, and re-layouts: 208 us -> 4.73 us
  matrix products: 63.8 us -> 0 us
  loops' own time: 42 us -> 0 us
  other arithmetic: 27.4 us -> 0 us
  between operations: 13.9 us -> 0.71 us
    psum x1 -> x0, blocking collectives: 322 us -> none  [body(): lax.psum(jnp.sum(grads.astype(f32) * z_vals.astype(f32), axis=0), 'ctx')]
    reduce_scatter x1 -> x0, waiting for transfers between devices: 116 us -> none  [body(): lax.psum_scatter(tap_sums[block_len:], 'ctx', scatter_dimension=0, tiled=...]
    reshape x34 -> x0, local copies, waits for them, and re-layouts: 114 us -> none  [the longest x33 112 us: toeplitz(): tiled[:, :block_len * (2 * block_len - 1)]]
    all_gather x2 -> x0, waiting for transfers between devices: 111 us -> none  [the longest x1 83.6 us: body(): g_piece = lax.all_gather(grads, 'ctx', axis=0, tiled=True)]
    dot_general x34 -> x0, matrix products: 63.8 us -> none  [the longest x32 61.4 us: backward(): jnp.einsum('gab,agc->bgc', tmat, remote_g, preferred_element_type=f32)]
    all_gather x1 -> x0, blocking collectives: 55.2 us -> none  [body(): all_taps = lax.all_gather(filters, 'ctx', axis=0, tiled=True)]
    dynamic_slice x66 -> x0, local copies, waits for them, and re-layouts: 50.9 us -> none  [the longest x32 27 us: span_step(): lax.dynamic_slice_in_dim(g_piece, position * block_len, block_len, 0)]
    another operation x65 -> x0, loops' own time: 42 us -> none  [the longest x1 40.6 us: body(): filtered, back_sum, tap_sums = lax.fori_loop(0, count, span_step, start)]
  transfers between devices with their start and end apart: 3 -> 0, of which waited for: 3 -> 0; matrix products, arithmetic and copies ran while one was open for 1% -> 0% of each run, Pallas kernels for 0% -> 0%
where the time goes in v1:
time: 48.3 us; the launch traced here: 47.9 us
  blocking collectives  39.6 us (82%)
  local copies, waits for them, and re-layouts  4.73 us (10%)
  Pallas kernels  2.85 us (6%)
  between operations  0.71 us (1%)
    all_to_all x2, blocking collectives, body(): packed = lax.all_to_all(packed, 'ctx', 0, 0, tiled=True)  39.6 us
    unnamed x22, local copies, waits for them, and re-layouts  4.73 us
    pallas_call x1, Pallas kernels, body(): pl.pallas_call(conv_body, out_shape=packed_shape, in_specs=[whole(space=p...  1.83 us

profile of v1, /device:TPU:56, one launch (start us, length us, event | category | flops | bytes accessed | tf_op | source)
XLA Modules:
  0.0 47.9 jit_solution(1572589683962367712)
XLA Ops:
  0.6 0.0 copy-start
  0.6 0.8 %copy-done = bf16[128,256]{1,0:T(8,128)(2,1)S(1)} copy-done((bf16[128,256]{1,0:T(8,128)(2,1)S(1)}, bf16[128,256]{1,0:T(8,128)(2,1)}, u32[]{:S(2)}) %copy-start) | copy-done | bytes 65560
  1.5 0.0 copy-start.2
  1.5 0.8 %copy-done.2 = bf16[128,256]{1,0:T(8,128)(2,1)S(1)} copy-done((bf16[128,256]{1,0:T(8,128)(2,1)S(1)}, bf16[128,256]{1,0:T(8,128)(2,1)}, u32[]{:S(2)}) %copy-start.2) | copy-done | bytes 65560
  2.3 0.0 copy-start.4
  2.3 0.8 %copy-done.4 = bf16[128,256]{1,0:T(8,128)(2,1)S(1)} copy-done((bf16[128,256]{1,0:T(8,128)(2,1)S(1)}, bf16[128,256]{1,0:T(8,128)(2,1)}, u32[]{:S(2)}) %copy-start.4) | copy-done | bytes 65560
  3.2 0.8 %copy-done.6 = bf16[128,256]{1,0:T(8,128)(2,1)S(1)} copy-done((bf16[128,256]{1,0:T(8,128)(2,1)S(1)}, bf16[128,256]{1,0:T(8,128)(2,1)}, u32[]{:S(2)}) %copy-start.6) | copy-done | bytes 65560
  4.0 0.7 %copy-done.8 = bf16[128,16]{0,1:T(8,128)(2,1)S(1)} copy-done((bf16[128,16]{0,1:T(8,128)(2,1)S(1)}, bf16[128,16]{0,1:T(8,128)(2,1)}, u32[]{:S(2)}) %copy-start.8) | copy-done | bytes 4120
  4.7 0.1 pack.1
  4.8 0.0 copy-start.10
  4.8 24.7 %all_to_all.10.packed = bf16[32,24,128]{2,1,0:T(8,128)(2,1)S(1)} all-to-all(bf16[32,24,128]{2,1,0:T(8,128)(2,1)S(1)} %pack.1), channel_id=1, replica_groups=mesh['ctx'=32,'ch'=16] {'ctx'}, dimensions={0} | all-to-all | bytes 393216 | tf_op jit(solution)/shard_map/all_to_all | solution.py:192
  29.5 0.0 copy-done.10
  29.5 1.8 %conv.1 = bf16[32,24,128]{2,1,0:T(8,128)(2,1)S(1)} custom-call(s32[16]{0:T(128)S(1)} %copy-done.10, bf16[32,24,128]{2,1,0:T(8,128)(2,1)S(1)} %all_to_all.10.packed), custom_call_target="tpu_custom_call" | custom-call | tf_op jit(solution)/shard_map/conv/pallas_call | solution.py:193
  31.3 0.0 copy-start.1
  31.3 0.0 copy-start.3
  31.3 0.0 copy-start.5
  31.3 0.0 copy-start.7
  31.4 14.9 %all_to_all.11.refs_5_ = bf16[32,24,128]{2,1,0:T(8,128)(2,1)S(1)} all-to-all(bf16[32,24,128]{2,1,0:T(8,128)(2,1)S(1)} %conv.1), channel_id=1, replica_groups=mesh['ctx'=32,'ch'=16] {'ctx'}, dimensions={0} | all-to-all | bytes 393216 | tf_op jit(solution)/shard_map/all_to_all | solution.py:205
  46.3 0.0 copy-done.1
  46.3 0.0 copy-done.3
  46.3 0.0 copy-done.5
  46.3 0.0 copy-done.7
  46.3 0.7 %copy-done.9 = f32[256]{0:T(256)S(1)} copy-done((f32[256]{0:T(256)S(1)}, f32[256]{0:T(256)}, u32[]{:S(2)}) %copy-start.9) | copy-done | bytes 1048
  46.9 0.9 %gate.1 = (bf16[128,256]{1,0:T(8,128)(2,1)}, bf16[128,256]{1,0:T(8,128)(2,1)}, bf16[128,256]{1,0:T(8,128)(2,1)}, bf16[128,256]{1,0:T(8,128)(2,1)}, f32[16,128]{1,0:T(8,128)}, /*index=5*/f32[1,256]{1,0:T(1,128)}) custom-call(bf16[128,256]{1,0:T(8,128)(2,1)S(1)} %copy-done.1, bf16[128,256]{1,0:T(8,128)(2,1)S(1)} %copy-done.3, bf16[128,256]{1,0:T(8,128)(2,1)S(1)} %copy-done.5, ...), custom_call_target="tpu_custom_call" | custom-call | tf_op jit(solution)/shard_map/gate/pallas_call | solution.py:207
  (3 shorter events, 0.0 us)
Async XLA Ops:
  0.6 0.8 %copy-start = (bf16[128,256]{1,0:T(8,128)(2,1)S(1)}, bf16[128,256]{1,0:T(8,128)(2,1)}, u32[]{:S(2)}) copy-start(bf16[128,256]{1,0:T(8,128)(2,1)} %refs_0_.1) | copy-start | bytes 196612
  1.5 0.8 %copy-start.2 = (bf16[128,256]{1,0:T(8,128)(2,1)S(1)}, bf16[128,256]{1,0:T(8,128)(2,1)}, u32[]{:S(2)}) copy-start(bf16[128,256]{1,0:T(8,128)(2,1)} %refs_1_.1) | copy-start | bytes 196612
  2.3 0.8 %copy-start.4 = (bf16[128,256]{1,0:T(8,128)(2,1)S(1)}, bf16[128,256]{1,0:T(8,128)(2,1)}, u32[]{:S(2)}) copy-start(bf16[128,256]{1,0:T(8,128)(2,1)} %refs_2_.1) | copy-start | bytes 196612
  3.2 0.8 %copy-start.6 = (bf16[128,256]{1,0:T(8,128)(2,1)S(1)}, bf16[128,256]{1,0:T(8,128)(2,1)}, u32[]{:S(2)}) copy-start(bf16[128,256]{1,0:T(8,128)(2,1)} %refs_3_.1) | copy-start | bytes 196612
  4.0 0.7 %copy-start.8 = (bf16[128,16]{0,1:T(8,128)(2,1)S(1)}, bf16[128,16]{0,1:T(8,128)(2,1)}, u32[]{:S(2)}) copy-start(bf16[128,16]{0,1:T(8,128)(2,1)} %param.11) | copy-start | bytes 12292
  4.8 24.7 %copy-start.10 = (s32[16]{0:T(128)S(1)}, s32[16]{0:T(128)}, u32[]{:S(2)}) copy-start(s32[16]{0:T(128)} %reaches.1) | copy-start | bytes 196
  31.3 15.0 %copy-start.1 = (bf16[128,256]{1,0:T(8,128)(2,1)S(1)}, bf16[128,256]{1,0:T(8,128)(2,1)}, u32[]{:S(2)}) copy-start(bf16[128,256]{1,0:T(8,128)(2,1)} %refs_0_.1) | copy-start | bytes 196612
  31.3 14.9 %copy-start.3 = (bf16[128,256]{1,0:T(8,128)(2,1)S(1)}, bf16[128,256]{1,0:T(8,128)(2,1)}, u32[]{:S(2)}) copy-start(bf16[128,256]{1,0:T(8,128)(2,1)} %refs_1_.1) | copy-start | bytes 196612
  31.3 14.9 %copy-start.5 = (bf16[128,256]{1,0:T(8,128)(2,1)S(1)}, bf16[128,256]{1,0:T(8,128)(2,1)}, u32[]{:S(2)}) copy-start(bf16[128,256]{1,0:T(8,128)(2,1)} %refs_2_.1) | copy-start | bytes 196612
  31.3 14.9 %copy-start.7 = (bf16[128,256]{1,0:T(8,128)(2,1)S(1)}, bf16[128,256]{1,0:T(8,128)(2,1)}, u32[]{:S(2)}) copy-start(bf16[128,256]{1,0:T(8,128)(2,1)} %refs_3_.1) | copy-start | bytes 196612
  46.3 0.7 %copy-start.9 = (f32[256]{0:T(256)S(1)}, f32[256]{0:T(256)}, u32[]{:S(2)}) copy-start(f32[256]{0:T(256)} %param.12) | copy-start | bytes 3076

commit v2 on v1

--- a/solution.py
+++ b/solution.py
@@ -1,3 +1,4 @@
+import functools
 import math
 
 import jax
@@ -32,12 +33,32 @@
     return (first.astype(F32) * second.astype(F32)).astype(BF16)
 
 
-def pack_body(query, key, value, cotangent, taps, packed):
-    spans = packed.shape[0]
-    block_len = query.shape[0]
-    z_rows = product(key[...], value[...]).astype(F32).T
-    g_rows = product(cotangent[...], query[...]).astype(F32).T
-    tap_rows = taps[...].astype(F32)
+def pack_body(query, key, value, cotangent, taps, gain, reaches, packed, gain_out, reach_out, q_buf, k_buf, v_buf, o_buf, t_buf, sems):
+    spans, _, block_len = packed.shape
+    moves = [
+        pltpu.make_async_copy(source, target, sems.at[place])
+        for place, (source, target) in enumerate(
+            [
+                (key, k_buf),
+                (value, v_buf),
+                (cotangent, o_buf),
+                (query, q_buf),
+                (taps, t_buf),
+                (gain, gain_out),
+                (reaches, reach_out),
+            ]
+        )
+    ]
+    for move in moves:
+        move.start()
+    moves[0].wait()
+    moves[1].wait()
+    z_rows = product(k_buf[...], v_buf[...]).astype(F32).T
+    moves[2].wait()
+    moves[3].wait()
+    g_rows = product(o_buf[...], q_buf[...]).astype(F32).T
+    moves[4].wait()
+    tap_rows = t_buf[...].astype(F32)
     for dest in range(spans):
         group = dest * 8 // GROUP
         tail = jnp.broadcast_to(tap_rows[group : group + 1], (8, block_len))
@@ -45,13 +66,20 @@
             [z_rows[dest * 8 : dest * 8 + 8], g_rows[dest * 8 : dest * 8 + 8], tail], axis=0
         )
         packed[dest] = tile.astype(BF16)
-
-
-def conv_body(reaches, packed, out, toep, shifted):
+    moves[5].wait()
+    moves[6].wait()
+
+
+def conv_body(scale, reaches, gain, packed, out, toep, shifted):
     spans, _, block_len = packed.shape
     wide = 2 * block_len
     half = spans // 2
-    reach = reaches[lax.axis_index("ctx") * 8 // GROUP]
+    owner = lax.axis_index("ctx")
+    place = lax.broadcasted_iota(jnp.int32, (1, reaches.shape[1]), 1)
+    reach = jnp.sum(jnp.where(place == owner * 8 // GROUP, reaches[...].astype(F32), 0.0), axis=1, keepdims=True)
+    place = lax.broadcasted_iota(jnp.int32, (8, gain.shape[1]), 1)
+    channel = lax.broadcasted_iota(jnp.int32, (8, gain.shape[1]), 0) + owner * 8
+    own_gain = jnp.sum(jnp.where(place == channel, gain[...], 0.0), axis=1, keepdims=True)
     row = lax.broadcasted_iota(jnp.int32, (block_len, block_len), 0)
     col = lax.broadcasted_iota(jnp.int32, (block_len, block_len), 1)
     upper = col >= row
@@ -60,7 +88,11 @@
     tiles = [packed[span].astype(F32) for span in range(spans)]
     z_list = [tile[0:8] for tile in tiles]
     g_list = [tile[8:16] for tile in tiles]
-    weights = [(offset < reach).astype(F32) for offset in range(spans)]
+    reach = jnp.broadcast_to(reach, (8, block_len))
+    weights = [
+        jnp.concatenate([jnp.where(reach > offset, 1.0, 0.0)] * (block_len // 8), axis=0)
+        for offset in range(spans)
+    ]
 
     toep[:, 0:block_len] = jnp.zeros((block_len, block_len), BF16)
     before = jnp.zeros((block_len, block_len), F32)
@@ -129,44 +161,52 @@
         tail = jnp.where(
             sub == 0, high, jnp.where(sub == 1, low, jnp.where(sub == 2, skip_high, skip_low))
         )
+        forth = forth * scale + own_gain * z_list[span]
+        back = back * scale + own_gain * g_flip[span * 8 : span * 8 + 8]
         out[span] = jnp.concatenate([forth, back, tail], axis=0).astype(BF16)
 
 
-def gate_body(scale, query, key, value, cotangent, gain, packed, mixed, query_grad, key_grad, value_grad, tap_grad, skip_grad):
+def gate_body(scale, query, key, value, cotangent, packed, mixed, query_grad, key_grad, value_grad, tap_grad, skip_grad, q_buf, o_buf, k_buf, v_buf, t_buf, s_buf, sems):
     spans, _, block_len = packed.shape
+    moves = []
+
+    def send(source, target):
+        moves.append(pltpu.make_async_copy(source, target, sems.at[len(moves)]))
+        moves[-1].start()
+
     tiles = [packed[span].astype(F32) for span in range(spans)]
     forth = jnp.concatenate([tile[0:8] for tile in tiles], axis=0).astype(BF16)
+    total = matmul_nt(eye(block_len, False), forth)
+    q_buf[...] = (query[...].astype(F32) * total).astype(BF16)
+    send(q_buf, mixed)
+    o_buf[...] = (cotangent[...].astype(F32) * total).astype(BF16)
+    send(o_buf, query_grad)
     back = jnp.concatenate([tile[8:16] for tile in tiles], axis=0).astype(BF16)
-    flip = eye(block_len, True)
-    filtered = matmul_nt(eye(block_len, False), forth) * scale
-    back_sum = matmul_nt(flip, back) * scale
-    q_val, k_val = query[...].astype(F32), key[...].astype(F32)
-    v_val, o_val = value[...].astype(F32), cotangent[...].astype(F32)
-    z_val = (k_val * v_val).astype(BF16).astype(F32)
-    g_val = (o_val * q_val).astype(BF16).astype(F32)
-    total = filtered + gain[...] * z_val
-    mixed[...] = (q_val * total).astype(BF16)
-    query_grad[...] = (o_val * total).astype(BF16)
-    back_total = back_sum + gain[...] * g_val
-    key_grad[...] = (back_total * v_val).astype(BF16)
-    value_grad[...] = (back_total * k_val).astype(BF16)
+    total = matmul_nt(eye(block_len, True), back)
+    k_buf[...] = (value[...].astype(F32) * total).astype(BF16)
+    send(k_buf, key_grad)
+    v_buf[...] = (key[...].astype(F32) * total).astype(BF16)
+    send(v_buf, value_grad)
 
     per_group = GROUP // 8
     for group in range(spans // per_group):
-        rows = tiles[group * per_group][16:24]
-        both = [rows[0:1], rows[1:2]]
-        for member in range(1, per_group):
+        line = jnp.zeros((1, block_len), F32)
+        for member in range(per_group):
             rows = tiles[group * per_group + member][16:24]
-            both = [both[0] + rows[0:1], both[1] + rows[1:2]]
-        tap_grad[group : group + 1] = (both[0] + both[1]) * scale
+            line = line + (rows[0:1] + rows[1:2])
+        t_buf[group : group + 1] = line * scale
+    send(t_buf, tap_grad)
 
     lane = lax.broadcasted_iota(jnp.int32, (1, block_len), 1)
-    for part in range(skip_grad.shape[1] // block_len):
+    for part in range(s_buf.shape[1] // block_len):
         line = jnp.zeros((1, block_len), F32)
         for place in range(block_len // 8):
             rows = tiles[part * (block_len // 8) + place][16:24]
             line = jnp.where(lane // 8 == place, rows[2:3] + rows[3:4], line)
-        skip_grad[:, part * block_len : (part + 1) * block_len] = line
+        s_buf[:, part * block_len : (part + 1) * block_len] = line
+    send(s_buf, skip_grad)
+    for move in moves:
+        move.wait()
 
 
 def whole(space=pltpu.VMEM):
@@ -181,19 +221,29 @@
     packed_shape = jax.ShapeDtypeStruct((spans, ROWS, block_len), BF16)
     params = pltpu.CompilerParams(vmem_limit_bytes=48 * 1024 * 1024)
 
-    packed = pl.pallas_call(
+    act = jax.ShapeDtypeStruct((block_len, local_width), BF16)
+    act_buf = pltpu.VMEM((block_len, local_width), BF16)
+
+    sources = [query_seq, key_seq, value_seq, out_grad, filters.T, skip_gain[None, :], reaches[None, :]]
+    packed, gain, reaches = pl.pallas_call(
         pack_body,
-        out_shape=packed_shape,
-        in_specs=[whole()] * 5,
-        out_specs=whole(),
+        out_shape=(
+            packed_shape,
+            jax.ShapeDtypeStruct((1, local_width), F32),
+            jax.ShapeDtypeStruct((1, local_groups), jnp.int32),
+        ),
+        in_specs=[whole(pltpu.HBM)] * 7,
+        out_specs=[whole()] * 3,
+        scratch_shapes=[act_buf] * 4
+        + [pltpu.VMEM((local_groups, block_len), BF16), pltpu.SemaphoreType.DMA((7,))],
         compiler_params=params,
         name="pack",
-    )(query_seq, key_seq, value_seq, out_grad, filters.T)
+    )(*[pltpu.with_memory_space_constraint(x, pltpu.HBM) for x in sources])
     packed = lax.all_to_all(packed, "ctx", 0, 0, tiled=True)
     packed = pl.pallas_call(
-        conv_body,
+        functools.partial(conv_body, scale),
         out_shape=packed_shape,
-        in_specs=[whole(space=pltpu.SMEM), whole()],
+        in_specs=[whole()] * 3,
         out_specs=whole(),
         scratch_shapes=[
             pltpu.VMEM((block_len, (spans + 1) * block_len), BF16),
@@ -201,24 +251,20 @@
         ],
         compiler_params=params,
         name="conv",
-    )(reaches, packed)
+    )(reaches, gain, packed)
     packed = lax.all_to_all(packed, "ctx", 0, 0, tiled=True)
-    act = jax.ShapeDtypeStruct((block_len, local_width), BF16)
+    tap_shape, skip_shape = (local_groups, block_len), (1, local_width)
     mixed, query_grad, key_grad, value_grad, tap_grad, skip_grad = pl.pallas_call(
-        lambda *refs: gate_body(scale, *refs),
-        out_shape=(
-            act,
-            act,
-            act,
-            act,
-            jax.ShapeDtypeStruct((local_groups, block_len), F32),
-            jax.ShapeDtypeStruct((1, local_width), F32),
-        ),
-        in_specs=[whole()] * 6,
-        out_specs=[whole()] * 6,
+        functools.partial(gate_body, scale),
+        out_shape=(act,) * 4
+        + (jax.ShapeDtypeStruct(tap_shape, F32), jax.ShapeDtypeStruct(skip_shape, F32)),
+        in_specs=[whole()] * 5,
+        out_specs=[whole(pltpu.HBM)] * 6,
+        scratch_shapes=[act_buf] * 4
+        + [pltpu.VMEM(tap_shape, F32), pltpu.VMEM(skip_shape, F32), pltpu.SemaphoreType.DMA((6,))],
         compiler_params=params,
         name="gate",
-    )(query_seq, key_seq, value_seq, out_grad, skip_gain[None, :], packed)
+    )(query_seq, key_seq, value_seq, out_grad, packed)
     return (mixed, query_grad, key_grad, value_grad, tap_grad.T, skip_grad[0])
 
 

time: 48.3 us -> 43.9 us (0.909)
  local copies, waits for them, and re-layouts: 4.73 us -> 0.03 us
  Pallas kernels: 2.85 us -> 3.45 us
    unnamed x22 -> x8, local copies, waits for them, and re-layouts: 4.73 us -> 0.03 us
    pallas_call x3, Pallas kernels: 2.85 us -> 3.45 us  [the longest x1 1.33 us: body(): pl.pallas_call(functools.partial(conv_body, scale), out_shape=packed_shap...]
where the time goes in v2:
time: 43.9 us; the launch traced here: 43.7 us
  blocking collectives  39.5 us (90%)
  Pallas kernels  3.45 us (8%)
  between operations  0.69 us (2%)
    all_to_all x2, blocking collectives, body(): packed = lax.all_to_all(packed, 'ctx', 0, 0, tiled=True)  39.5 us
    pallas_call x1, Pallas kernels, body(): pl.pallas_call(functools.partial(conv_body, scale), out_shape=packed_shap...  1.33 us
    pallas_call x1, Pallas kernels, body(): pl.pallas_call(pack_body, out_shape=(packed_shape, jax.ShapeDtypeStruct((...  1.16 us
    pallas_call x1, Pallas kernels, body(): pl.pallas_call(functools.partial(gate_body, scale), out_shape=(act,) * 4...  0.95 us

profile of v2, /device:TPU:56, one launch (start us, length us, event | category | flops | bytes accessed | tf_op | source)
XLA Modules:
  0.0 43.7 jit_solution(13444048362596868004)
XLA Ops:
  0.6 1.2 %pack.1 = (bf16[32,24,128]{2,1,0:T(8,128)(2,1)S(1)}, f32[1,256]{1,0:T(1,128)S(1)}, s32[1,16]{1,0:T(1,128)S(1)}) custom-call(bf16[128,256]{1,0:T(8,128)(2,1)} %query.3, bf16[128,256]{1,0:T(8,128)(2,1)} %key.3, bf16[128,256]{1,0:T(8,128)(2,1)} %value.3, bf16[128,256]{1,0:T(8,128)(2,1)} %cotangent.3, bf16[16,128]{1,0:T(8,128)(2,1)} %bitcast.5, ...), custom_call_target="tpu_custom_call" | custom-call | tf_op jit(solution)/shard_map/pack/pallas_call | solution.py:228
  1.8 24.7 %all_to_all.10.packed = bf16[32,24,128]{2,1,0:T(8,128)(2,1)S(1)} all-to-all(bf16[32,24,128]{2,1,0:T(8,128)(2,1)S(1)} %get-tuple-element.17), channel_id=1, replica_groups=mesh['ctx'=32,'ch'=16] {'ctx'}, dimensions={0} | all-to-all | bytes 393216 | tf_op jit(solution)/shard_map/all_to_all | solution.py:242
  26.5 1.3 %conv.1 = bf16[32,24,128]{2,1,0:T(8,128)(2,1)S(1)} custom-call(s32[1,16]{1,0:T(1,128)S(1)} %get-tuple-element.15.reaches, f32[1,256]{1,0:T(1,128)S(1)} %get-tuple-element.16.gain, bf16[32,24,128]{2,1,0:T(8,128)(2,1)S(1)} %all_to_all.10.packed), custom_call_target="tpu_custom_call" | custom-call | tf_op jit(solution)/shard_map/conv/pallas_call | solution.py:243
  27.8 0.0 copy-start
  27.8 0.0 copy-start.1
  27.8 0.0 copy-start.2
  27.8 0.0 copy-start.3
  27.9 14.8 %all_to_all.11.packed = bf16[32,24,128]{2,1,0:T(8,128)(2,1)S(1)} all-to-all(bf16[32,24,128]{2,1,0:T(8,128)(2,1)S(1)} %conv.1), channel_id=1, replica_groups=mesh['ctx'=32,'ch'=16] {'ctx'}, dimensions={0} | all-to-all | bytes 393216 | tf_op jit(solution)/shard_map/all_to_all | solution.py:255
  42.7 0.0 copy-done
  42.7 0.0 copy-done.1
  42.7 0.0 copy-done.2
  42.7 0.0 copy-done.3
  42.7 0.9 %gate.1 = (bf16[128,256]{1,0:T(8,128)(2,1)}, bf16[128,256]{1,0:T(8,128)(2,1)}, bf16[128,256]{1,0:T(8,128)(2,1)}, bf16[128,256]{1,0:T(8,128)(2,1)}, f32[16,128]{1,0:T(8,128)}, /*index=5*/f32[1,256]{1,0:T(1,128)}) custom-call(bf16[128,256]{1,0:T(8,128)(2,1)S(1)} %copy-done, bf16[128,256]{1,0:T(8,128)(2,1)S(1)} %copy-done.1, bf16[128,256]{1,0:T(8,128)(2,1)S(1)} %copy-done.2, ...), custom_call_target="tpu_custom_call" | custom-call | tf_op jit(solution)/shard_map/gate/pallas_call | solution.py:257
Async XLA Ops:
  27.8 14.9 %copy-start = (bf16[128,256]{1,0:T(8,128)(2,1)S(1)}, bf16[128,256]{1,0:T(8,128)(2,1)}, u32[]{:S(2)}) copy-start(bf16[128,256]{1,0:T(8,128)(2,1)} %query.3) | copy-start | bytes 196612
  27.8 14.9 %copy-start.1 = (bf16[128,256]{1,0:T(8,128)(2,1)S(1)}, bf16[128,256]{1,0:T(8,128)(2,1)}, u32[]{:S(2)}) copy-start(bf16[128,256]{1,0:T(8,128)(2,1)} %key.3) | copy-start | bytes 196612
  27.8 14.9 %copy-start.2 = (bf16[128,256]{1,0:T(8,128)(2,1)S(1)}, bf16[128,256]{1,0:T(8,128)(2,1)}, u32[]{:S(2)}) copy-start(bf16[128,256]{1,0:T(8,128)(2,1)} %value.3) | copy-start | bytes 196612
  27.8 14.9 %copy-start.3 = (bf16[128,256]{1,0:T(8,128)(2,1)S(1)}, bf16[128,256]{1,0:T(8,128)(2,1)}, u32[]{:S(2)}) copy-start(bf16[128,256]{1,0:T(8,128)(2,1)} %cotangent.3) | copy-start | bytes 196612

commit v3 on v2

--- a/solution.py
+++ b/solution.py
@@ -9,7 +9,8 @@
 from jax.sharding import PartitionSpec as P
 
 GROUP = 16
-ROWS = 24
+OWN = 8
+ROWS = 2 * OWN + 2
 F32 = jnp.float32
 BF16 = jnp.bfloat16
 
@@ -34,7 +35,7 @@
 
 
 def pack_body(query, key, value, cotangent, taps, gain, reaches, packed, gain_out, reach_out, q_buf, k_buf, v_buf, o_buf, t_buf, sems):
-    spans, _, block_len = packed.shape
+    spans = packed.shape[0] // ROWS
     moves = [
         pltpu.make_async_copy(source, target, sems.at[place])
         for place, (source, target) in enumerate(
@@ -60,18 +61,19 @@
     moves[4].wait()
     tap_rows = t_buf[...].astype(F32)
     for dest in range(spans):
-        group = dest * 8 // GROUP
-        tail = jnp.broadcast_to(tap_rows[group : group + 1], (8, block_len))
-        tile = jnp.concatenate(
-            [z_rows[dest * 8 : dest * 8 + 8], g_rows[dest * 8 : dest * 8 + 8], tail], axis=0
-        )
-        packed[dest] = tile.astype(BF16)
+        here = slice(dest * OWN, (dest + 1) * OWN)
+        base = dest * ROWS
+        tile = jnp.concatenate([z_rows[here], g_rows[here]], axis=0)
+        packed[base : base + 2 * OWN] = tile.astype(BF16)
+        group = dest * OWN // GROUP
+        tail = jnp.broadcast_to(tap_rows[group : group + 1], (2, tap_rows.shape[1]))
+        packed[base + 2 * OWN : base + ROWS] = tail.astype(BF16)
     moves[5].wait()
     moves[6].wait()
 
 
 def conv_body(scale, reaches, gain, packed, out, toep, shifted):
-    spans, _, block_len = packed.shape
+    spans, block_len = packed.shape[0] // ROWS, packed.shape[1]
     wide = 2 * block_len
     half = spans // 2
     owner = lax.axis_index("ctx")
@@ -85,9 +87,10 @@
     upper = col >= row
     flip = eye(block_len, True)
 
-    tiles = [packed[span].astype(F32) for span in range(spans)]
-    z_list = [tile[0:8] for tile in tiles]
-    g_list = [tile[8:16] for tile in tiles]
+    tiles = [packed[span * ROWS : span * ROWS + 2 * OWN].astype(F32) for span in range(spans)]
+    z_list = [tile[:OWN] for tile in tiles]
+    g_list = [tile[OWN:] for tile in tiles]
+    taps = [packed[(span + 1) * ROWS - 2 : (span + 1) * ROWS].astype(F32)[:1] for span in range(spans)]
     reach = jnp.broadcast_to(reach, (8, block_len))
     weights = [
         jnp.concatenate([jnp.where(reach > offset, 1.0, 0.0)] * (block_len // 8), axis=0)
@@ -97,7 +100,7 @@
     toep[:, 0:block_len] = jnp.zeros((block_len, block_len), BF16)
     before = jnp.zeros((block_len, block_len), F32)
     for offset in range(spans):
-        window = jnp.broadcast_to(tiles[offset][16:17], (block_len, block_len))
+        window = jnp.broadcast_to(taps[offset], (block_len, block_len))
         turned = pltpu.roll(window, 0, 1, stride=1, stride_axis=0)
         block = jnp.where(upper, turned, before) * weights[offset]
         toep[:, (offset + 1) * block_len : (offset + 2) * block_len] = block.astype(BF16)
@@ -146,8 +149,8 @@
     lane = lax.broadcasted_iota(jnp.int32, (8, block_len), 1)
     sub = lax.broadcasted_iota(jnp.int32, (8, block_len), 0)
     skip_row = jnp.sum(jnp.where(lane % 8 == sub, skip, 0.0), axis=0, keepdims=True)
-    skip_high = skip_row.astype(BF16).astype(F32)
-    skip_low = skip_row - skip_high
+    high = skip_row.astype(BF16).astype(F32)
+    skip_row = jnp.where(lane[:1] < block_len // 2, high, skip_row - high)
 
     for span in range(spans):
         pair, side = span // 2, span % 2
@@ -156,25 +159,23 @@
         pair, side = mirror // 2, mirror % 2
         back = acc[pair * 16 + 8 : pair * 16 + 16, side * block_len : (side + 1) * block_len]
         sums = jnp.sum(jnp.where(col <= row, turned[span], turned[span + 1]), axis=0, keepdims=True)
-        high = sums.astype(BF16).astype(F32)
-        low = sums - high
-        tail = jnp.where(
-            sub == 0, high, jnp.where(sub == 1, low, jnp.where(sub == 2, skip_high, skip_low))
-        )
         forth = forth * scale + own_gain * z_list[span]
         back = back * scale + own_gain * g_flip[span * 8 : span * 8 + 8]
-        out[span] = jnp.concatenate([forth, back, tail], axis=0).astype(BF16)
+        base = span * ROWS
+        out[base : base + 2 * OWN] = jnp.concatenate([forth, back], axis=0).astype(BF16)
+        out[base + 2 * OWN : base + ROWS] = jnp.concatenate([sums, skip_row], axis=0).astype(BF16)
 
 
 def gate_body(scale, query, key, value, cotangent, packed, mixed, query_grad, key_grad, value_grad, tap_grad, skip_grad, q_buf, o_buf, k_buf, v_buf, t_buf, s_buf, sems):
-    spans, _, block_len = packed.shape
+    spans, block_len = packed.shape[0] // ROWS, packed.shape[1]
     moves = []
 
     def send(source, target):
         moves.append(pltpu.make_async_copy(source, target, sems.at[len(moves)]))
         moves[-1].start()
 
-    tiles = [packed[span].astype(F32) for span in range(spans)]
+    tiles = [packed[span * ROWS : span * ROWS + 2 * OWN].astype(F32) for span in range(spans)]
+    tails = [packed[(span + 1) * ROWS - 2 : (span + 1) * ROWS].astype(F32) for span in range(spans)]
     forth = jnp.concatenate([tile[0:8] for tile in tiles], axis=0).astype(BF16)
     total = matmul_nt(eye(block_len, False), forth)
     q_buf[...] = (query[...].astype(F32) * total).astype(BF16)
@@ -192,17 +193,20 @@
     for group in range(spans // per_group):
         line = jnp.zeros((1, block_len), F32)
         for member in range(per_group):
-            rows = tiles[group * per_group + member][16:24]
-            line = line + (rows[0:1] + rows[1:2])
+            line = line + tails[group * per_group + member][0:1]
         t_buf[group : group + 1] = line * scale
     send(t_buf, tap_grad)
 
     lane = lax.broadcasted_iota(jnp.int32, (1, block_len), 1)
+    per_row = block_len // OWN
     for part in range(s_buf.shape[1] // block_len):
         line = jnp.zeros((1, block_len), F32)
-        for place in range(block_len // 8):
-            rows = tiles[part * (block_len // 8) + place][16:24]
-            line = jnp.where(lane // 8 == place, rows[2:3] + rows[3:4], line)
+        other = jnp.zeros((1, block_len), F32)
+        for place in range(per_row):
+            piece = tails[part * per_row + place][1:2]
+            line = jnp.where(lane // OWN == place, piece, line)
+            other = jnp.where(lane // OWN == (place + per_row // 2) % per_row, piece, other)
+        line = line + pltpu.roll(other, block_len // 2, 1)
         s_buf[:, part * block_len : (part + 1) * block_len] = line
     send(s_buf, skip_grad)
     for move in moves:
@@ -213,48 +217,50 @@
     return pl.BlockSpec(memory_space=space)
 
 
-def body(query_seq, key_seq, value_seq, out_grad, filters, skip_gain, reaches):
-    block_len, local_width = query_seq.shape
-    spans = lax.axis_size("ctx")
-    local_groups = local_width // GROUP
-    scale = 1.0 / math.sqrt(block_len * spans)
-    packed_shape = jax.ShapeDtypeStruct((spans, ROWS, block_len), BF16)
-    params = pltpu.CompilerParams(vmem_limit_bytes=48 * 1024 * 1024)
-
-    act = jax.ShapeDtypeStruct((block_len, local_width), BF16)
-    act_buf = pltpu.VMEM((block_len, local_width), BF16)
-
-    sources = [query_seq, key_seq, value_seq, out_grad, filters.T, skip_gain[None, :], reaches[None, :]]
-    packed, gain, reaches = pl.pallas_call(
+PARAMS = pltpu.CompilerParams(vmem_limit_bytes=48 * 1024 * 1024)
+
+
+def pack(query_seq, key_seq, value_seq, out_grad, taps, gain, reaches, spans):
+    block_len, width = query_seq.shape
+    act_buf = pltpu.VMEM((block_len, width), BF16)
+    sources = [query_seq, key_seq, value_seq, out_grad, taps, gain, reaches]
+    return pl.pallas_call(
         pack_body,
         out_shape=(
-            packed_shape,
-            jax.ShapeDtypeStruct((1, local_width), F32),
-            jax.ShapeDtypeStruct((1, local_groups), jnp.int32),
+            jax.ShapeDtypeStruct((spans * ROWS, block_len), BF16),
+            jax.ShapeDtypeStruct(gain.shape, gain.dtype),
+            jax.ShapeDtypeStruct(reaches.shape, reaches.dtype),
         ),
         in_specs=[whole(pltpu.HBM)] * 7,
         out_specs=[whole()] * 3,
-        scratch_shapes=[act_buf] * 4
-        + [pltpu.VMEM((local_groups, block_len), BF16), pltpu.SemaphoreType.DMA((7,))],
-        compiler_params=params,
+        scratch_shapes=[act_buf] * 4 + [pltpu.VMEM(taps.shape, BF16), pltpu.SemaphoreType.DMA((7,))],
+        compiler_params=PARAMS,
         name="pack",
     )(*[pltpu.with_memory_space_constraint(x, pltpu.HBM) for x in sources])
-    packed = lax.all_to_all(packed, "ctx", 0, 0, tiled=True)
-    packed = pl.pallas_call(
+
+
+def conv(reaches, gain, packed, scale):
+    spans, block_len = packed.shape[0] // ROWS, packed.shape[1]
+    return pl.pallas_call(
         functools.partial(conv_body, scale),
-        out_shape=packed_shape,
+        out_shape=jax.ShapeDtypeStruct(packed.shape, BF16),
         in_specs=[whole()] * 3,
         out_specs=whole(),
         scratch_shapes=[
             pltpu.VMEM((block_len, (spans + 1) * block_len), BF16),
             pltpu.VMEM((spans * 16, 2 * block_len), BF16),
         ],
-        compiler_params=params,
+        compiler_params=PARAMS,
         name="conv",
     )(reaches, gain, packed)
-    packed = lax.all_to_all(packed, "ctx", 0, 0, tiled=True)
-    tap_shape, skip_shape = (local_groups, block_len), (1, local_width)
-    mixed, query_grad, key_grad, value_grad, tap_grad, skip_grad = pl.pallas_call(
+
+
+def gate(query_seq, key_seq, value_seq, out_grad, packed, scale):
+    block_len, width = query_seq.shape
+    act = jax.ShapeDtypeStruct((block_len, width), BF16)
+    act_buf = pltpu.VMEM((block_len, width), BF16)
+    tap_shape, skip_shape = (width // GROUP, block_len), (1, width)
+    return pl.pallas_call(
         functools.partial(gate_body, scale),
         out_shape=(act,) * 4
         + (jax.ShapeDtypeStruct(tap_shape, F32), jax.ShapeDtypeStruct(skip_shape, F32)),
@@ -262,10 +268,26 @@
         out_specs=[whole(pltpu.HBM)] * 6,
         scratch_shapes=[act_buf] * 4
         + [pltpu.VMEM(tap_shape, F32), pltpu.VMEM(skip_shape, F32), pltpu.SemaphoreType.DMA((6,))],
-        compiler_params=params,
+        compiler_params=PARAMS,
         name="gate",
     )(query_seq, key_seq, value_seq, out_grad, packed)
-    return (mixed, query_grad, key_grad, value_grad, tap_grad.T, skip_grad[0])
+
+
+def exchange(packed, spans):
+    paired = packed.reshape(spans, ROWS // 2, 2, packed.shape[1])
+    return lax.all_to_all(paired, "ctx", 0, 0, tiled=True).reshape(packed.shape)
+
+
+def body(query_seq, key_seq, value_seq, out_grad, filters, skip_gain, reaches):
+    spans = lax.axis_size("ctx")
+    scale = 1.0 / math.sqrt(query_seq.shape[0] * spans)
+    acts = (query_seq, key_seq, value_seq, out_grad)
+    packed, gain, reaches = pack(*acts, filters.T, skip_gain[None, :], reaches[None, :], spans)
+    packed = exchange(packed, spans)
+    packed = conv(reaches, gain, packed, scale)
+    packed = exchange(packed, spans)
+    *grads, tap_grad, skip_grad = gate(*acts, packed, scale)
+    return (*grads, tap_grad.T, skip_grad[0])
 
 
 def solution(mesh):

time: 43.9 us -> 42.5 us (0.968)
  blocking collectives: 39.5 us -> 38 us
    all_to_all x2, blocking collectives: 39.5 us -> 38 us  [exchange(): return lax.all_to_all(paired, 'ctx', 0, 0, tiled=True).reshape(packed.shape)]
where the time goes in v3:
time: 42.5 us; the launch traced here: 42.2 us
  blocking collectives  38 us (89%)
  Pallas kernels  3.49 us (8%)
  between operations  0.69 us (2%)
    all_to_all x2, blocking collectives, exchange(): return lax.all_to_all(paired, 'ctx', 0, 0, tiled=True).reshape(packed.shape)  38 us
    pallas_call x1, Pallas kernels, conv(): pl.pallas_call(functools.partial(conv_body, scale), out_shape=jax.ShapeDt...  1.34 us
    pallas_call x1, Pallas kernels, pack(): pl.pallas_call(pack_body, out_shape=(jax.ShapeDtypeStruct((spans * ROWS,...  1.19 us
    pallas_call x1, Pallas kernels, gate(): pl.pallas_call(functools.partial(gate_body, scale), out_shape=(act,) * 4...  0.96 us

profile of v3, /device:TPU:56, one launch (start us, length us, event | category | flops | bytes accessed | tf_op | source)
XLA Modules:
  0.0 42.2 jit_solution(15700344980300667604)
XLA Ops:
  0.6 1.2 %pack.1 = (bf16[576,128]{1,0:T(8,128)(2,1)S(1)}, f32[1,256]{1,0:T(1,128)S(1)}, s32[1,16]{1,0:T(1,128)S(1)}) custom-call(bf16[128,256]{1,0:T(8,128)(2,1)} %query.3, bf16[128,256]{1,0:T(8,128)(2,1)} %key.3, bf16[128,256]{1,0:T(8,128)(2,1)} %value.3, bf16[128,256]{1,0:T(8,128)(2,1)} %cotangent.3, bf16[16,128]{1,0:T(8,128)(2,1)} %bitcast.13, f32[1,256]{1,0:T(1,128)} %bitcast.14, ...), custom_call_target="tpu_custom_call" | custom-call | tf_op jit(solution)/shard_map/pack/pallas_call | solution.py:227
  1.8 23.8 %all_to_all.10 = bf16[32,9,2,128]{3,2,1,0:T(2,128)(2,1)S(1)} all-to-all(bf16[32,9,2,128]{3,2,1,0:T(2,128)(2,1)S(1)} %bitcast.12), channel_id=1, replica_groups=mesh['ctx'=32,'ch'=16] {'ctx'}, dimensions={0} | all-to-all | bytes 294912 | tf_op jit(solution)/shard_map/all_to_all | solution.py:278
  25.6 1.3 %conv.1 = bf16[576,128]{1,0:T(8,128)(2,1)S(1)} custom-call(s32[1,16]{1,0:T(1,128)S(1)} %get-tuple-element.15.reaches, f32[1,256]{1,0:T(1,128)S(1)} %get-tuple-element.16.gain, bf16[576,128]{1,0:T(8,128)(2,1)S(1)} %bitcast.10), custom_call_target="tpu_custom_call" | custom-call | tf_op jit(solution)/shard_map/conv/pallas_call | solution.py:244
  26.9 0.0 copy-start
  26.9 0.0 copy-start.1
  27.0 0.0 copy-start.2
  27.0 0.0 copy-start.3
  27.0 14.2 %all_to_all.11 = bf16[32,9,2,128]{3,2,1,0:T(2,128)(2,1)S(1)} all-to-all(bf16[32,9,2,128]{3,2,1,0:T(2,128)(2,1)S(1)} %bitcast.11), channel_id=1, replica_groups=mesh['ctx'=32,'ch'=16] {'ctx'}, dimensions={0} | all-to-all | bytes 294912 | tf_op jit(solution)/shard_map/all_to_all | solution.py:278
  41.2 0.0 copy-done
  41.2 0.0 copy-done.1
  41.2 0.0 copy-done.2
  41.2 0.0 copy-done.3
  41.2 1.0 %gate.1 = (bf16[128,256]{1,0:T(8,128)(2,1)}, bf16[128,256]{1,0:T(8,128)(2,1)}, bf16[128,256]{1,0:T(8,128)(2,1)}, bf16[128,256]{1,0:T(8,128)(2,1)}, f32[16,128]{1,0:T(8,128)}, /*index=5*/f32[1,256]{1,0:T(1,128)}) custom-call(bf16[128,256]{1,0:T(8,128)(2,1)S(1)} %copy-done, bf16[128,256]{1,0:T(8,128)(2,1)S(1)} %copy-done.1, bf16[128,256]{1,0:T(8,128)(2,1)S(1)} %copy-done.2, ...), custom_call_target="tpu_custom_call" | custom-call | tf_op jit(solution)/shard_map/gate/pallas_call | solution.py:263
Async XLA Ops:
  26.9 14.3 %copy-start = (bf16[128,256]{1,0:T(8,128)(2,1)S(1)}, bf16[128,256]{1,0:T(8,128)(2,1)}, u32[]{:S(2)}) copy-start(bf16[128,256]{1,0:T(8,128)(2,1)} %query.3) | copy-start | bytes 196612
  26.9 14.3 %copy-start.1 = (bf16[128,256]{1,0:T(8,128)(2,1)S(1)}, bf16[128,256]{1,0:T(8,128)(2,1)}, u32[]{:S(2)}) copy-start(bf16[128,256]{1,0:T(8,128)(2,1)} %key.3) | copy-start | bytes 196612
  27.0 14.3 %copy-start.2 = (bf16[128,256]{1,0:T(8,128)(2,1)S(1)}, bf16[128,256]{1,0:T(8,128)(2,1)}, u32[]{:S(2)}) copy-start(bf16[128,256]{1,0:T(8,128)(2,1)} %value.3) | copy-start | bytes 196612
  27.0 14.3 %copy-start.3 = (bf16[128,256]{1,0:T(8,128)(2,1)S(1)}, bf16[128,256]{1,0:T(8,128)(2,1)}, u32[]{:S(2)}) copy-start(bf16[128,256]{1,0:T(8,128)(2,1)} %cotangent.3) | copy-start | bytes 196612

commit v4 on v3

--- a/solution.py
+++ b/solution.py
@@ -50,29 +50,31 @@
             ]
         )
     ]
-    for move in moves:
-        move.start()
+    for place in (0, 1, 4, 2, 3, 5, 6):
+        moves[place].start()
     moves[0].wait()
     moves[1].wait()
-    z_rows = product(k_buf[...], v_buf[...]).astype(F32).T
+    z_rows = product(k_buf[...], v_buf[...]).T.astype(F32)
+    moves[4].wait()
+    tap_rows = t_buf[...].astype(F32)
+    for dest in range(spans):
+        base = dest * ROWS
+        group = dest * OWN // GROUP
+        tail = jnp.broadcast_to(tap_rows[group : group + 1], (2, tap_rows.shape[1]))
+        packed[base + 2 * OWN : base + ROWS] = tail.astype(BF16)
     moves[2].wait()
     moves[3].wait()
-    g_rows = product(o_buf[...], q_buf[...]).astype(F32).T
-    moves[4].wait()
-    tap_rows = t_buf[...].astype(F32)
+    g_rows = product(o_buf[...], q_buf[...]).T.astype(F32)
     for dest in range(spans):
         here = slice(dest * OWN, (dest + 1) * OWN)
         base = dest * ROWS
         tile = jnp.concatenate([z_rows[here], g_rows[here]], axis=0)
         packed[base : base + 2 * OWN] = tile.astype(BF16)
-        group = dest * OWN // GROUP
-        tail = jnp.broadcast_to(tap_rows[group : group + 1], (2, tap_rows.shape[1]))
-        packed[base + 2 * OWN : base + ROWS] = tail.astype(BF16)
     moves[5].wait()
     moves[6].wait()
 
 
-def conv_body(scale, reaches, gain, packed, out, toep, shifted):
+def conv_body(scale, reaches, gain, packed, out, toep, shifted, acc_ref):
     spans, block_len = packed.shape[0] // ROWS, packed.shape[1]
     wide = 2 * block_len
     half = spans // 2
@@ -97,18 +99,13 @@
         for offset in range(spans)
     ]
 
-    toep[:, 0:block_len] = jnp.zeros((block_len, block_len), BF16)
-    before = jnp.zeros((block_len, block_len), F32)
-    for offset in range(spans):
-        window = jnp.broadcast_to(taps[offset], (block_len, block_len))
-        turned = pltpu.roll(window, 0, 1, stride=1, stride_axis=0)
-        block = jnp.where(upper, turned, before) * weights[offset]
-        toep[:, (offset + 1) * block_len : (offset + 2) * block_len] = block.astype(BF16)
-        before = turned
-
     g_all = jnp.concatenate(g_list, axis=0).astype(BF16)
     g_flip = matmul(g_all, flip)
-
+    z_flip = matmul(jnp.concatenate(z_list, axis=0).astype(BF16), flip)
+    z_down = jnp.concatenate([jnp.zeros((8, block_len), F32), z_flip[:-8]], axis=0)
+    shifted[0 : spans * 8] = jnp.zeros((spans * 8, wide), BF16)
+    shifted[spans * 8 : spans * 16] = jnp.concatenate([z_flip, z_down], axis=1).astype(BF16)
+    g_turn = jnp.concatenate(g_list, axis=0).T.astype(BF16)
     parts = []
     for pair in range(half):
         first = 2 * pair
@@ -116,31 +113,38 @@
         low, high = (spans - 1 - first) * 8, (spans - 2 - first) * 8
         parts.append(jnp.concatenate([g_flip[low : low + 8], g_flip[high : high + 8]], axis=1))
     data = jnp.concatenate(parts, axis=0).astype(BF16)
+
+    toep[:, 0:block_len] = jnp.zeros((block_len, block_len), BF16)
+    before = jnp.zeros((block_len, block_len), F32)
     acc = None
-    for offset in range(half):
-        base = 2 * offset * block_len
+    sum_rows = []
+    last = None
+    for pair in range(half):
+        for offset in (2 * pair, 2 * pair + 1):
+            window = jnp.broadcast_to(taps[offset], (block_len, block_len))
+            turned = pltpu.roll(window, 0, 1, stride=1, stride_axis=0)
+            block = jnp.where(col >= row, turned, before)
+            toep[:, (offset + 1) * block_len : (offset + 2) * block_len] = block.astype(BF16) * weights[offset].astype(BF16)
+            before = turned
+        base = 2 * pair * block_len
         block = jnp.concatenate(
             [toep[:, base + block_len : base + block_len + wide], toep[:, base : base + wide]], axis=0
         )
-        term = matmul(data[: (half - offset) * 16], block)
+        term = matmul(data[: (half - pair) * 16], block)
         if acc is None:
-            acc = term
+            acc = acc_ref
+            acc[...] = term
         else:
-            acc = jnp.concatenate([acc[: offset * 16], acc[offset * 16 :] + term], axis=0)
-
-    z_flip = matmul(jnp.concatenate(z_list, axis=0).astype(BF16), flip)
-    z_down = jnp.concatenate([jnp.zeros((8, block_len), F32), z_flip[:-8]], axis=0)
-    shifted[0 : spans * 8] = jnp.zeros((spans * 8, wide), BF16)
-    shifted[spans * 8 : spans * 16] = jnp.concatenate([z_flip, z_down], axis=1).astype(BF16)
-    g_turn = jnp.concatenate(g_list, axis=0).T.astype(BF16)
-    turned = []
-    for pair in range(half):
+            acc[pair * 16 :] += term
         start = spans * 8 - 16 * pair
         prods = matmul(g_turn, shifted[start : start + spans * 8])
         for side in range(2):
             own = prods[:, side * block_len : (side + 1) * block_len] * weights[2 * pair + side]
-            turned.append(pltpu.roll(own, 1, 1, stride=1, stride_axis=0))
-    turned.append(jnp.zeros((block_len, block_len), F32))
+            own = pltpu.roll(own, 1, 1, stride=1, stride_axis=0)
+            if last is not None:
+                sum_rows.append(jnp.sum(jnp.where(col <= row, last, own), axis=0, keepdims=True))
+            last = own
+    sum_rows.append(jnp.sum(jnp.where(col <= row, last, 0.0), axis=0, keepdims=True))
 
     skip = jnp.zeros((8, block_len), F32)
     for span in range(spans):
@@ -158,7 +162,7 @@
         mirror = spans - 1 - span
         pair, side = mirror // 2, mirror % 2
         back = acc[pair * 16 + 8 : pair * 16 + 16, side * block_len : (side + 1) * block_len]
-        sums = jnp.sum(jnp.where(col <= row, turned[span], turned[span + 1]), axis=0, keepdims=True)
+        sums = sum_rows[span]
         forth = forth * scale + own_gain * z_list[span]
         back = back * scale + own_gain * g_flip[span * 8 : span * 8 + 8]
         base = span * ROWS
@@ -176,13 +180,12 @@
 
     tiles = [packed[span * ROWS : span * ROWS + 2 * OWN].astype(F32) for span in range(spans)]
     tails = [packed[(span + 1) * ROWS - 2 : (span + 1) * ROWS].astype(F32) for span in range(spans)]
-    forth = jnp.concatenate([tile[0:8] for tile in tiles], axis=0).astype(BF16)
-    total = matmul_nt(eye(block_len, False), forth)
+    total = jnp.concatenate([tile[:OWN] for tile in tiles], axis=0).T
     q_buf[...] = (query[...].astype(F32) * total).astype(BF16)
     send(q_buf, mixed)
     o_buf[...] = (cotangent[...].astype(F32) * total).astype(BF16)
     send(o_buf, query_grad)
-    back = jnp.concatenate([tile[8:16] for tile in tiles], axis=0).astype(BF16)
+    back = jnp.concatenate([tile[OWN:] for tile in tiles], axis=0).astype(BF16)
     total = matmul_nt(eye(block_len, True), back)
     k_buf[...] = (value[...].astype(F32) * total).astype(BF16)
     send(k_buf, key_grad)
@@ -249,6 +252,7 @@
         scratch_shapes=[
             pltpu.VMEM((block_len, (spans + 1) * block_len), BF16),
             pltpu.VMEM((spans * 16, 2 * block_len), BF16),
+            pltpu.VMEM((spans * 8, 2 * block_len), F32),
         ],
         compiler_params=PARAMS,
         name="conv",

time: 42.5 us -> 42.1 us (level)
  no operation moved by 1% of the time
where the time goes in v4:
time: 42.1 us; the launch traced here: 41.9 us
  blocking collectives  38 us (90%)
  Pallas kernels  3.16 us (8%)
  between operations  0.69 us (2%)
    all_to_all x2, blocking collectives, exchange(): return lax.all_to_all(paired, 'ctx', 0, 0, tiled=True).reshape(packed.shape)  38 us
    pallas_call x1, Pallas kernels, conv(): pl.pallas_call(functools.partial(conv_body, scale), out_shape=jax.ShapeDt...  1.15 us
    pallas_call x1, Pallas kernels, pack(): pl.pallas_call(pack_body, out_shape=(jax.ShapeDtypeStruct((spans * ROWS,...  1.11 us
    pallas_call x1, Pallas kernels, gate(): pl.pallas_call(functools.partial(gate_body, scale), out_shape=(act,) * 4...  0.89 us

profile of v4, /device:TPU:56, one launch (start us, length us, event | category | flops | bytes accessed | tf_op | source)
XLA Modules:
  0.0 41.9 jit_solution(3967343237001087797)
XLA Ops:
  0.6 1.1 %pack.1 = (bf16[576,128]{1,0:T(8,128)(2,1)S(1)}, f32[1,256]{1,0:T(1,128)S(1)}, s32[1,16]{1,0:T(1,128)S(1)}) custom-call(bf16[128,256]{1,0:T(8,128)(2,1)} %query.3, bf16[128,256]{1,0:T(8,128)(2,1)} %key.3, bf16[128,256]{1,0:T(8,128)(2,1)} %value.3, bf16[128,256]{1,0:T(8,128)(2,1)} %cotangent.3, bf16[16,128]{1,0:T(8,128)(2,1)} %bitcast.13, f32[1,256]{1,0:T(1,128)} %bitcast.14, ...), custom_call_target="tpu_custom_call" | custom-call | tf_op jit(solution)/shard_map/pack/pallas_call | solution.py:230
  1.7 23.8 %all_to_all.10 = bf16[32,9,2,128]{3,2,1,0:T(2,128)(2,1)S(1)} all-to-all(bf16[32,9,2,128]{3,2,1,0:T(2,128)(2,1)S(1)} %bitcast.12), channel_id=1, replica_groups=mesh['ctx'=32,'ch'=16] {'ctx'}, dimensions={0} | all-to-all | bytes 294912 | tf_op jit(solution)/shard_map/all_to_all | solution.py:282
  25.5 1.2 %conv.1 = bf16[576,128]{1,0:T(8,128)(2,1)S(1)} custom-call(s32[1,16]{1,0:T(1,128)S(1)} %get-tuple-element.15.reaches, f32[1,256]{1,0:T(1,128)S(1)} %get-tuple-element.16.gain, bf16[576,128]{1,0:T(8,128)(2,1)S(1)} %bitcast.10), custom_call_target="tpu_custom_call" | custom-call | tf_op jit(solution)/shard_map/conv/pallas_call | solution.py:247
  26.7 0.0 copy-start
  26.7 0.0 copy-start.1
  26.7 0.0 copy-start.2
  26.7 0.0 copy-start.3
  26.7 14.2 %all_to_all.11 = bf16[32,9,2,128]{3,2,1,0:T(2,128)(2,1)S(1)} all-to-all(bf16[32,9,2,128]{3,2,1,0:T(2,128)(2,1)S(1)} %bitcast.11), channel_id=1, replica_groups=mesh['ctx'=32,'ch'=16] {'ctx'}, dimensions={0} | all-to-all | bytes 294912 | tf_op jit(solution)/shard_map/all_to_all | solution.py:282
  41.0 0.0 copy-done
  41.0 0.0 copy-done.1
  41.0 0.0 copy-done.2
  41.0 0.0 copy-done.3
  41.0 0.9 %gate.1 = (bf16[128,256]{1,0:T(8,128)(2,1)}, bf16[128,256]{1,0:T(8,128)(2,1)}, bf16[128,256]{1,0:T(8,128)(2,1)}, bf16[128,256]{1,0:T(8,128)(2,1)}, f32[16,128]{1,0:T(8,128)}, /*index=5*/f32[1,256]{1,0:T(1,128)}) custom-call(bf16[128,256]{1,0:T(8,128)(2,1)S(1)} %copy-done, bf16[128,256]{1,0:T(8,128)(2,1)S(1)} %copy-done.1, bf16[128,256]{1,0:T(8,128)(2,1)S(1)} %copy-done.2, ...), custom_call_target="tpu_custom_call" | custom-call | tf_op jit(solution)/shard_map/gate/pallas_call | solution.py:267
Async XLA Ops:
  26.7 14.3 %copy-start = (bf16[128,256]{1,0:T(8,128)(2,1)S(1)}, bf16[128,256]{1,0:T(8,128)(2,1)}, u32[]{:S(2)}) copy-start(bf16[128,256]{1,0:T(8,128)(2,1)} %query.3) | copy-start | bytes 196612
  26.7 14.3 %copy-start.1 = (bf16[128,256]{1,0:T(8,128)(2,1)S(1)}, bf16[128,256]{1,0:T(8,128)(2,1)}, u32[]{:S(2)}) copy-start(bf16[128,256]{1,0:T(8,128)(2,1)} %key.3) | copy-start | bytes 196612
  26.7 14.3 %copy-start.2 = (bf16[128,256]{1,0:T(8,128)(2,1)S(1)}, bf16[128,256]{1,0:T(8,128)(2,1)}, u32[]{:S(2)}) copy-start(bf16[128,256]{1,0:T(8,128)(2,1)} %value.3) | copy-start | bytes 196612
  26.7 14.3 %copy-start.3 = (bf16[128,256]{1,0:T(8,128)(2,1)S(1)}, bf16[128,256]{1,0:T(8,128)(2,1)}, u32[]{:S(2)}) copy-start(bf16[128,256]{1,0:T(8,128)(2,1)} %cotangent.3) | copy-start | bytes 196612

commit v5 on v4

--- a/solution.py
+++ b/solution.py
@@ -74,7 +74,7 @@
     moves[6].wait()
 
 
-def conv_body(scale, reaches, gain, packed, out, toep, shifted, acc_ref):
+def conv_body(scale, reaches, gain, packed, out, shifted, acc_ref):
     spans, block_len = packed.shape[0] // ROWS, packed.shape[1]
     wide = 2 * block_len
     half = spans // 2
@@ -114,21 +114,22 @@
         parts.append(jnp.concatenate([g_flip[low : low + 8], g_flip[high : high + 8]], axis=1))
     data = jnp.concatenate(parts, axis=0).astype(BF16)
 
-    toep[:, 0:block_len] = jnp.zeros((block_len, block_len), BF16)
     before = jnp.zeros((block_len, block_len), F32)
+    odd = jnp.zeros((block_len, block_len), BF16)
     acc = None
     sum_rows = []
     last = None
     for pair in range(half):
+        blocks = [odd]
         for offset in (2 * pair, 2 * pair + 1):
             window = jnp.broadcast_to(taps[offset], (block_len, block_len))
             turned = pltpu.roll(window, 0, 1, stride=1, stride_axis=0)
-            block = jnp.where(col >= row, turned, before)
-            toep[:, (offset + 1) * block_len : (offset + 2) * block_len] = block.astype(BF16) * weights[offset].astype(BF16)
+            block = jnp.where(col >= row, turned, before).astype(BF16)
+            blocks.append(block * weights[offset].astype(BF16))
             before = turned
-        base = 2 * pair * block_len
+        odd = blocks[2]
         block = jnp.concatenate(
-            [toep[:, base + block_len : base + block_len + wide], toep[:, base : base + wide]], axis=0
+            [jnp.concatenate(blocks[1:], axis=1), jnp.concatenate(blocks[:2], axis=1)], axis=0
         )
         term = matmul(data[: (half - pair) * 16], block)
         if acc is None:
@@ -225,7 +226,6 @@
 
 def pack(query_seq, key_seq, value_seq, out_grad, taps, gain, reaches, spans):
     block_len, width = query_seq.shape
-    act_buf = pltpu.VMEM((block_len, width), BF16)
     sources = [query_seq, key_seq, value_seq, out_grad, taps, gain, reaches]
     return pl.pallas_call(
         pack_body,
@@ -233,10 +233,11 @@
             jax.ShapeDtypeStruct((spans * ROWS, block_len), BF16),
             jax.ShapeDtypeStruct(gain.shape, gain.dtype),
             jax.ShapeDtypeStruct(reaches.shape, reaches.dtype),
-        ),
+        )
+        + (jax.ShapeDtypeStruct((block_len, width), BF16),) * 4,
         in_specs=[whole(pltpu.HBM)] * 7,
-        out_specs=[whole()] * 3,
-        scratch_shapes=[act_buf] * 4 + [pltpu.VMEM(taps.shape, BF16), pltpu.SemaphoreType.DMA((7,))],
+        out_specs=[whole()] * 7,
+        scratch_shapes=[pltpu.VMEM(taps.shape, BF16), pltpu.SemaphoreType.DMA((7,))],
         compiler_params=PARAMS,
         name="pack",
     )(*[pltpu.with_memory_space_constraint(x, pltpu.HBM) for x in sources])
@@ -250,7 +251,6 @@
         in_specs=[whole()] * 3,
         out_specs=whole(),
         scratch_shapes=[
-            pltpu.VMEM((block_len, (spans + 1) * block_len), BF16),
             pltpu.VMEM((spans * 16, 2 * block_len), BF16),
             pltpu.VMEM((spans * 8, 2 * block_len), F32),
         ],
@@ -286,7 +286,7 @@
     spans = lax.axis_size("ctx")
     scale = 1.0 / math.sqrt(query_seq.shape[0] * spans)
     acts = (query_seq, key_seq, value_seq, out_grad)
-    packed, gain, reaches = pack(*acts, filters.T, skip_gain[None, :], reaches[None, :], spans)
+    packed, gain, reaches, *acts = pack(*acts, filters.T, skip_gain[None, :], reaches[None, :], spans)
     packed = exchange(packed, spans)
     packed = conv(reaches, gain, packed, scale)
     packed = exchange(packed, spans)

time: 42.1 us -> 41.9 us (level)
  no operation moved by 1% of the time
where the time goes in v5:
time: 41.9 us; the launch traced here: 41.7 us
  blocking collectives  37.9 us (90%)
  Pallas kernels  3.14 us (7%)
  between operations  0.65 us (2%)
    all_to_all x2, blocking collectives, exchange(): return lax.all_to_all(paired, 'ctx', 0, 0, tiled=True).reshape(packed.shape)  37.9 us
    pallas_call x1, Pallas kernels, conv(): pl.pallas_call(functools.partial(conv_body, scale), out_shape=jax.ShapeDt...  1.14 us
    pallas_call x1, Pallas kernels, pack(): pl.pallas_call(pack_body, out_shape=(jax.ShapeDtypeStruct((spans * ROWS,...  1.11 us
    pallas_call x1, Pallas kernels, gate(): pl.pallas_call(functools.partial(gate_body, scale), out_shape=(act,) * 4...  0.89 us

profile of v5, /device:TPU:56, one launch (start us, length us, event | category | flops | bytes accessed | tf_op | source)
XLA Modules:
  0.0 41.7 jit_solution(13025834044504970708)
XLA Ops:
  0.6 1.1 %pack.1 = (bf16[576,128]{1,0:T(8,128)(2,1)S(1)}, f32[1,256]{1,0:T(1,128)S(1)}, s32[1,16]{1,0:T(1,128)S(1)}, bf16[128,256]{1,0:T(8,128)(2,1)S(1)}, bf16[128,256]{...) custom-call(bf16[128,256]{1,0:T(8,128)(2,1)} %query.1, bf16[128,256]{1,0:T(8,128)(2,1)} %key.1, ...), custom_call_target="tpu_custom_call" | custom-call | tf_op jit(solution)/shard_map/pack/pallas_call | solution.py:230
  1.8 23.8 %all_to_all.10 = bf16[32,9,2,128]{3,2,1,0:T(2,128)(2,1)S(1)} all-to-all(bf16[32,9,2,128]{3,2,1,0:T(2,128)(2,1)S(1)} %bitcast.12), channel_id=1, replica_groups=mesh['ctx'=32,'ch'=16] {'ctx'}, dimensions={0} | all-to-all | bytes 294912 | tf_op jit(solution)/shard_map/all_to_all | solution.py:282
  25.5 1.1 %conv.1 = bf16[576,128]{1,0:T(8,128)(2,1)S(1)} custom-call(s32[1,16]{1,0:T(1,128)S(1)} %get-tuple-element.23.reaches, f32[1,256]{1,0:T(1,128)S(1)} %get-tuple-element.24.gain, bf16[576,128]{1,0:T(8,128)(2,1)S(1)} %bitcast.10), custom_call_target="tpu_custom_call" | custom-call | tf_op jit(solution)/shard_map/conv/pallas_call | solution.py:248
  26.7 14.1 %all_to_all.11 = bf16[32,9,2,128]{3,2,1,0:T(2,128)(2,1)S(1)} all-to-all(bf16[32,9,2,128]{3,2,1,0:T(2,128)(2,1)S(1)} %bitcast.11), channel_id=1, replica_groups=mesh['ctx'=32,'ch'=16] {'ctx'}, dimensions={0} | all-to-all | bytes 294912 | tf_op jit(solution)/shard_map/all_to_all | solution.py:282
  40.8 0.9 %gate.1 = (bf16[128,256]{1,0:T(8,128)(2,1)}, bf16[128,256]{1,0:T(8,128)(2,1)}, bf16[128,256]{1,0:T(8,128)(2,1)}, bf16[128,256]{1,0:T(8,128)(2,1)}, f32[16,128]{1,0:T(8,128)}, /*index=5*/f32[1,256]{1,0:T(1,128)}) custom-call(bf16[128,256]{1,0:T(8,128)(2,1)S(1)} %get-tuple-element.19.query, bf16[128,256]{1,0:T(8,128)(2,1)S(1)} %get-tuple-element.20.key, ...), custom_call_target="tpu_custom_call" | custom-call | tf_op jit(solution)/shard_map/gate/pallas_call | solution.py:267

commit v6 on v5

--- a/solution.py
+++ b/solution.py
@@ -106,6 +106,16 @@
     shifted[0 : spans * 8] = jnp.zeros((spans * 8, wide), BF16)
     shifted[spans * 8 : spans * 16] = jnp.concatenate([z_flip, z_down], axis=1).astype(BF16)
     g_turn = jnp.concatenate(g_list, axis=0).T.astype(BF16)
+    skip = jnp.zeros((8, block_len), F32)
+    for span in range(spans):
+        skip = skip + z_list[span] * g_list[span]
+    skip = jnp.sum(skip, axis=1, keepdims=True)
+    lane = lax.broadcasted_iota(jnp.int32, (8, block_len), 1)
+    sub = lax.broadcasted_iota(jnp.int32, (8, block_len), 0)
+    skip_row = jnp.sum(jnp.where(lane % 8 == sub, skip, 0.0), axis=0, keepdims=True)
+    high = skip_row.astype(BF16).astype(F32)
+    skip_row = jnp.where(lane[:1] < block_len // 2, high, skip_row - high)
+
     parts = []
     for pair in range(half):
         first = 2 * pair
@@ -147,16 +157,6 @@
             last = own
     sum_rows.append(jnp.sum(jnp.where(col <= row, last, 0.0), axis=0, keepdims=True))
 
-    skip = jnp.zeros((8, block_len), F32)
-    for span in range(spans):
-        skip = skip + z_list[span] * g_list[span]
-    skip = jnp.sum(skip, axis=1, keepdims=True)
-    lane = lax.broadcasted_iota(jnp.int32, (8, block_len), 1)
-    sub = lax.broadcasted_iota(jnp.int32, (8, block_len), 0)
-    skip_row = jnp.sum(jnp.where(lane % 8 == sub, skip, 0.0), axis=0, keepdims=True)
-    high = skip_row.astype(BF16).astype(F32)
-    skip_row = jnp.where(lane[:1] < block_len // 2, high, skip_row - high)
-
     for span in range(spans):
         pair, side = span // 2, span % 2
         forth = acc[pair * 16 : pair * 16 + 8, side * block_len : (side + 1) * block_len]

time: 41.9 us -> 41.8 us (level)
  no operation moved by 1% of the time
where the time goes in v6:
time: 41.8 us; the launch traced here: 41.6 us
  blocking collectives  37.9 us (91%)
  Pallas kernels  3.11 us (7%)
  between operations  0.65 us (2%)
    all_to_all x2, blocking collectives, exchange(): return lax.all_to_all(paired, 'ctx', 0, 0, tiled=True).reshape(packed.shape)  37.9 us
    pallas_call x1, Pallas kernels, pack(): pl.pallas_call(pack_body, out_shape=(jax.ShapeDtypeStruct((spans * ROWS,...  1.11 us
    pallas_call x1, Pallas kernels, conv(): pl.pallas_call(functools.partial(conv_body, scale), out_shape=jax.ShapeDt...  1.11 us
    pallas_call x1, Pallas kernels, gate(): pl.pallas_call(functools.partial(gate_body, scale), out_shape=(act,) * 4...  0.89 us

profile of v6, /device:TPU:56, one launch (start us, length us, event | category | flops | bytes accessed | tf_op | source)
XLA Modules:
  0.0 41.6 jit_solution(17782527480737055120)
XLA Ops:
  0.6 1.1 %pack.1 = (bf16[576,128]{1,0:T(8,128)(2,1)S(1)}, f32[1,256]{1,0:T(1,128)S(1)}, s32[1,16]{1,0:T(1,128)S(1)}, bf16[128,256]{1,0:T(8,128)(2,1)S(1)}, bf16[128,256]{...) custom-call(bf16[128,256]{1,0:T(8,128)(2,1)} %query.1, bf16[128,256]{1,0:T(8,128)(2,1)} %key.1, ...), custom_call_target="tpu_custom_call" | custom-call | tf_op jit(solution)/shard_map/pack/pallas_call | solution.py:230
  1.8 23.8 %all_to_all.10 = bf16[32,9,2,128]{3,2,1,0:T(2,128)(2,1)S(1)} all-to-all(bf16[32,9,2,128]{3,2,1,0:T(2,128)(2,1)S(1)} %bitcast.12), channel_id=1, replica_groups=mesh['ctx'=32,'ch'=16] {'ctx'}, dimensions={0} | all-to-all | bytes 294912 | tf_op jit(solution)/shard_map/all_to_all | solution.py:282
  25.5 1.1 %conv.1 = bf16[576,128]{1,0:T(8,128)(2,1)S(1)} custom-call(s32[1,16]{1,0:T(1,128)S(1)} %get-tuple-element.23.reaches, f32[1,256]{1,0:T(1,128)S(1)} %get-tuple-element.24.gain, bf16[576,128]{1,0:T(8,128)(2,1)S(1)} %bitcast.10), custom_call_target="tpu_custom_call" | custom-call | tf_op jit(solution)/shard_map/conv/pallas_call | solution.py:248
  26.6 14.1 %all_to_all.11 = bf16[32,9,2,128]{3,2,1,0:T(2,128)(2,1)S(1)} all-to-all(bf16[32,9,2,128]{3,2,1,0:T(2,128)(2,1)S(1)} %bitcast.11), channel_id=1, replica_groups=mesh['ctx'=32,'ch'=16] {'ctx'}, dimensions={0} | all-to-all | bytes 294912 | tf_op jit(solution)/shard_map/all_to_all | solution.py:282
  40.7 0.9 %gate.1 = (bf16[128,256]{1,0:T(8,128)(2,1)}, bf16[128,256]{1,0:T(8,128)(2,1)}, bf16[128,256]{1,0:T(8,128)(2,1)}, bf16[128,256]{1,0:T(8,128)(2,1)}, f32[16,128]{1,0:T(8,128)}, /*index=5*/f32[1,256]{1,0:T(1,128)}) custom-call(bf16[128,256]{1,0:T(8,128)(2,1)S(1)} %get-tuple-element.19.query, bf16[128,256]{1,0:T(8,128)(2,1)S(1)} %get-tuple-element.20.key, ...), custom_call_target="tpu_custom_call" | custom-call | tf_op jit(solution)/shard_map/gate/pallas_call | solution.py:267

commit v7 on v5

--- a/solution.py
+++ b/solution.py
@@ -55,6 +55,8 @@
     moves[0].wait()
     moves[1].wait()
     z_rows = product(k_buf[...], v_buf[...]).T.astype(F32)
+    for dest in range(spans):
+        packed[dest * ROWS : dest * ROWS + OWN] = z_rows[dest * OWN : (dest + 1) * OWN].astype(BF16)
     moves[4].wait()
     tap_rows = t_buf[...].astype(F32)
     for dest in range(spans):
@@ -68,8 +70,7 @@
     for dest in range(spans):
         here = slice(dest * OWN, (dest + 1) * OWN)
         base = dest * ROWS
-        tile = jnp.concatenate([z_rows[here], g_rows[here]], axis=0)
-        packed[base : base + 2 * OWN] = tile.astype(BF16)
+        packed[base + OWN : base + 2 * OWN] = g_rows[here].astype(BF16)
     moves[5].wait()
     moves[6].wait()
 

time: 41.9 us -> 41.9 us (level)
  no operation moved by 1% of the time
where the time goes in v7:
time: 41.9 us; the launch traced here: 41.7 us
  blocking collectives  37.9 us (90%)
  Pallas kernels  3.14 us (7%)
  between operations  0.65 us (2%)
    all_to_all x2, blocking collectives, exchange(): return lax.all_to_all(paired, 'ctx', 0, 0, tiled=True).reshape(packed.shape)  37.9 us
    pallas_call x1, Pallas kernels, conv(): pl.pallas_call(functools.partial(conv_body, scale), out_shape=jax.ShapeDt...  1.14 us
    pallas_call x1, Pallas kernels, pack(): pl.pallas_call(pack_body, out_shape=(jax.ShapeDtypeStruct((spans * ROWS,...  1.11 us
    pallas_call x1, Pallas kernels, gate(): pl.pallas_call(functools.partial(gate_body, scale), out_shape=(act,) * 4...  0.89 us

profile of v7, /device:TPU:56, one launch (start us, length us, event | category | flops | bytes accessed | tf_op | source)
XLA Modules:
  0.0 41.7 jit_solution(7112184027397521815)
XLA Ops:
  0.6 1.1 %pack.1 = (bf16[576,128]{1,0:T(8,128)(2,1)S(1)}, f32[1,256]{1,0:T(1,128)S(1)}, s32[1,16]{1,0:T(1,128)S(1)}, bf16[128,256]{1,0:T(8,128)(2,1)S(1)}, bf16[128,256]{...) custom-call(bf16[128,256]{1,0:T(8,128)(2,1)} %query.1, bf16[128,256]{1,0:T(8,128)(2,1)} %key.1, ...), custom_call_target="tpu_custom_call" | custom-call | tf_op jit(solution)/shard_map/pack/pallas_call | solution.py:231
  1.7 23.8 %all_to_all.10 = bf16[32,9,2,128]{3,2,1,0:T(2,128)(2,1)S(1)} all-to-all(bf16[32,9,2,128]{3,2,1,0:T(2,128)(2,1)S(1)} %bitcast.12), channel_id=1, replica_groups=mesh['ctx'=32,'ch'=16] {'ctx'}, dimensions={0} | all-to-all | bytes 294912 | tf_op jit(solution)/shard_map/all_to_all | solution.py:283
  25.5 1.1 %conv.1 = bf16[576,128]{1,0:T(8,128)(2,1)S(1)} custom-call(s32[1,16]{1,0:T(1,128)S(1)} %get-tuple-element.23.reaches, f32[1,256]{1,0:T(1,128)S(1)} %get-tuple-element.24.gain, bf16[576,128]{1,0:T(8,128)(2,1)S(1)} %bitcast.10), custom_call_target="tpu_custom_call" | custom-call | tf_op jit(solution)/shard_map/conv/pallas_call | solution.py:249
  26.7 14.1 %all_to_all.11 = bf16[32,9,2,128]{3,2,1,0:T(2,128)(2,1)S(1)} all-to-all(bf16[32,9,2,128]{3,2,1,0:T(2,128)(2,1)S(1)} %bitcast.11), channel_id=1, replica_groups=mesh['ctx'=32,'ch'=16] {'ctx'}, dimensions={0} | all-to-all | bytes 294912 | tf_op jit(solution)/shard_map/all_to_all | solution.py:283
  40.8 0.9 %gate.1 = (bf16[128,256]{1,0:T(8,128)(2,1)}, bf16[128,256]{1,0:T(8,128)(2,1)}, bf16[128,256]{1,0:T(8,128)(2,1)}, bf16[128,256]{1,0:T(8,128)(2,1)}, f32[16,128]{1,0:T(8,128)}, /*index=5*/f32[1,256]{1,0:T(1,128)}) custom-call(bf16[128,256]{1,0:T(8,128)(2,1)S(1)} %get-tuple-element.19.query, bf16[128,256]{1,0:T(8,128)(2,1)S(1)} %get-tuple-element.20.key, ...), custom_call_target="tpu_custom_call" | custom-call | tf_op jit(solution)/shard_map/gate/pallas_call | solution.py:268
